TPU v7x, 512 devices: a whole 4x4x16 slice. The times are simulated.
512 devices in a mesh: region: 32 (over x_hi, z), mode: 16 (over y, x_lo, core).
Axes of the slice: x: 4 (x_hi: 2, x_lo: 2; x = x_hi * 2 + x_lo), y: 4, z: 16, core: 2. Of those that a mesh axis runs over, the one named last changes fastest.
Arguments:
- measured: float32 [64, 256, 256], P('region'), may hold values from 0.05 to 20
- probe_modes: float32 [2, 16, 256, 256], P(None, 'mode'), may hold values from -1.5 to 1.5
- object_bands: float32 [2, 4096, 512], P(None, 'region'), may hold values from -4.2 to 4.2
- scan_offsets: int32 [64, 2], replicated, may hold values from 0 to 3839, as said below
- band_owner: int32 [32], replicated, may hold values from 0 to 31, each once
Outputs:
- probe_out: float32 [2, 16, 256, 256], P(None, 'mode')
- object_out: float32 [2, 4096, 512], P(None, 'region')
Inputs may be any that keep to these rules, and one draw needn't show every extreme that they name: `scan_offsets`: every frame covers rows r to r + 255 within the bands r // 128 to r // 128 + 2; no band is covered by two frames of one region (frames f * 2 to f * 2 + 1 form region f).
All inputs are finite; a program needn't handle non-finite values.
Results may differ from a plain program's by a relative error of at most 0.0001.
Values sent between devices are 32-bit elements; how exact they have to be, the bound alone decides.
A program may use at most 64 MiB of HBM per device.

v0:
```python
import math

import jax
import jax.numpy as jnp
from jax import lax
from jax.sharding import PartitionSpec as P

intensity_offset = 0.1
probe_damping = 1.0
object_damping = 1.0
highest = lax.Precision.HIGHEST


def fourier_tables(length, orientation):
    positions = jnp.arange(length, dtype=jnp.int32)
    product = positions[:, None] * positions[None, :] % length
    angles = product.astype(jnp.float32) * (2.0 * math.pi / length)
    normalizer = 1.0 / math.sqrt(length)
    cosine_table = jnp.cos(angles) * normalizer
    sine_table = orientation * jnp.sin(angles) * normalizer
    return (cosine_table, cosine_table + sine_table, sine_table - cosine_table)


def left_product(matrix, planes):
    return jnp.einsum("jk,...kl->...jl", matrix, planes, precision=highest)


def right_product(planes, matrix):
    return jnp.einsum("...jk,kl->...jl", planes, matrix, precision=highest)


def transform(real_part, imag_part, tables):
    cosine_table, plus_table, minus_table = tables
    common = left_product(cosine_table, real_part + imag_part)
    left_real = common - left_product(plus_table, imag_part)
    left_imag = common + left_product(minus_table, real_part)
    common = right_product(left_real + left_imag, cosine_table)
    right_real = common - right_product(left_imag, plus_table)
    right_imag = common + right_product(left_real, minus_table)
    return (right_real, right_imag)


def wave_change(probe_modes, windows, root_measured, forward_tables, inverse_tables):
    probe_real = probe_modes[0][None]
    probe_imag = probe_modes[1][None]
    window_real = windows[:, 0][:, None]
    window_imag = windows[:, 1][:, None]
    exit_real = probe_real * window_real - probe_imag * window_imag
    exit_imag = probe_real * window_imag + probe_imag * window_real
    wave_real, wave_imag = transform(exit_real, exit_imag, forward_tables)
    local_sum = jnp.sum(wave_real * wave_real + wave_imag * wave_imag, axis=1)
    summed = lax.psum(local_sum, "mode")
    factor = (root_measured / jnp.sqrt(summed + intensity_offset) - 1.0)[:, None]
    return transform(wave_real * factor, wave_imag * factor, inverse_tables)


def body(measured, probe_modes, object_bands, scan_offsets, band_owner):
    frames_dev = measured.shape[0]
    length = measured.shape[1]
    band_rows = length // 2
    width_total = object_bands.shape[2]
    region_count = lax.axis_size("region")
    mode_count = lax.axis_size("mode")
    share_rows = band_rows // mode_count
    region_index = lax.axis_index("region")
    mode_index = lax.axis_index("mode")
    forward_tables = fourier_tables(length, -1.0)
    inverse_tables = fourier_tables(length, 1.0)
    region_range = jnp.arange(region_count, dtype=jnp.int32)
    own_band = jnp.sum(region_range * (band_owner == region_index).astype(jnp.int32))
    first_rows = scan_offsets[:, 0]
    anchors = first_rows // band_rows
    touched = (
        ((anchors <= own_band) & (own_band <= anchors + 2))
        .astype(jnp.int32)
        .reshape(region_count, frames_dev)
    )
    source_has = jnp.sum(touched, axis=1)
    source_column = jnp.sum(touched * scan_offsets[:, 1].reshape(region_count, frames_dev), axis=1)
    own_rows = lax.dynamic_slice_in_dim(object_bands, mode_index * share_rows, share_rows, 1)

    def cut_piece(column, present):
        return lax.dynamic_slice_in_dim(own_rows, column, length, 2) * present.astype(jnp.float32)

    outgoing = jax.vmap(cut_piece)(source_column, source_has)
    incoming = lax.all_to_all(outgoing, "region", split_axis=0, concat_axis=0, tiled=True)
    own_offsets = lax.dynamic_slice_in_dim(scan_offsets, region_index * frames_dev, frames_dev, 0)
    own_anchor = own_offsets[:, 0] // band_rows
    own_lead = own_offsets[:, 0] - own_anchor * band_rows
    needed = (own_anchor[:, None] + jnp.arange(3, dtype=jnp.int32)[None, :]).reshape(-1)
    holder = jnp.sum(
        band_owner[None, :] * (needed[:, None] == region_range[None, :]).astype(jnp.int32), axis=1
    )
    selector = (holder[None, :] == region_range[:, None]).astype(jnp.float32)
    chosen = jnp.einsum("sp,scrn->pcrn", selector, incoming, precision=highest)
    assembled = lax.all_gather(chosen, "mode", axis=2, tiled=True)
    stacked = assembled.reshape(frames_dev, 3, 2, band_rows, length)
    stacked_rows = jnp.concatenate([stacked[:, 0], stacked[:, 1], stacked[:, 2]], axis=2)
    windows = jax.vmap(
        lambda frame_rows, lead_rows: lax.dynamic_slice_in_dim(frame_rows, lead_rows, length, 1)
    )(stacked_rows, own_lead)
    root_measured = jnp.sqrt(measured)
    window_real = windows[:, 0][:, None]
    window_imag = windows[:, 1][:, None]
    object_power = jnp.sum(windows[:, 0] ** 2 + windows[:, 1] ** 2, axis=0)
    change_real, change_imag = wave_change(
        probe_modes, windows, root_measured, forward_tables, inverse_tables
    )
    grad_real = jnp.sum(window_real * change_real + window_imag * change_imag, axis=0)
    grad_imag = jnp.sum(window_real * change_imag - window_imag * change_real, axis=0)
    gradient = jnp.stack([grad_real, grad_imag])
    gradient, power_total = lax.psum((gradient, object_power), "region")
    probe_modes = probe_modes + gradient / (power_total + probe_damping)
    change_real, change_imag = wave_change(
        probe_modes, windows, root_measured, forward_tables, inverse_tables
    )
    probe_real = probe_modes[0][None]
    probe_imag = probe_modes[1][None]
    numer_real = jnp.sum(probe_real * change_real + probe_imag * change_imag, axis=1)
    numer_imag = jnp.sum(probe_real * change_imag - probe_imag * change_real, axis=1)
    mode_power = jnp.sum(probe_modes[0] ** 2 + probe_modes[1] ** 2, axis=0)
    power_modes = lax.psum(mode_power, "mode")

    def split_pieces(frame_rows, lead_rows):
        return jnp.stack(
            [
                lax.dynamic_slice_in_dim(
                    frame_rows, band_rows - lead_rows + piece_number * band_rows, band_rows, 1
                )
                for piece_number in range(3)
            ]
        )

    channels = jnp.stack([numer_real, numer_imag], axis=1)
    padded = jnp.pad(channels, ((0, 0), (0, 0), (band_rows, band_rows), (0, 0)))
    pieces = jax.vmap(split_pieces)(padded, own_lead)
    row_pieces = lax.psum_scatter(pieces, "mode", scatter_dimension=3, tiled=True)
    power_frames = jnp.broadcast_to(
        jnp.pad(power_modes, ((band_rows, band_rows), (0, 0)))[None, None],
        (frames_dev, 1, 2 * band_rows + length, length),
    )
    power_pieces = jax.vmap(split_pieces)(power_frames, own_lead)
    power_share = lax.dynamic_slice_in_dim(power_pieces, mode_index * share_rows, share_rows, 3)
    row_pieces = jnp.concatenate([row_pieces, power_share], axis=2)
    channel_count = row_pieces.shape[2]
    flat_pieces = row_pieces.reshape(frames_dev * 3, channel_count, share_rows, length)
    outgoing_update = jnp.einsum("sp,pcrn->scrn", selector, flat_pieces, precision=highest)
    arriving = lax.all_to_all(outgoing_update, "region", split_axis=0, concat_axis=0, tiled=True)

    def place_piece(piece_rows, column):
        blank = jnp.zeros((piece_rows.shape[0], share_rows, width_total), jnp.float32)
        return lax.dynamic_update_slice_in_dim(blank, piece_rows, column, 2)

    placed = jnp.sum(jax.vmap(place_piece)(arriving, source_column), axis=0)
    density_rows = placed[2]
    new_rows = own_rows + placed[0:2] / (density_rows + object_damping)
    object_out = lax.all_gather(new_rows, "mode", axis=1, tiled=True)
    return (probe_modes, object_out)


def solution(mesh):
    in_specs = (
        P("region", None, None),
        P(None, "mode", None, None),
        P(None, "region", None),
        P(),
        P(),
    )
    out_specs = (P(None, "mode", None, None), P(None, "region", None))
    return jax.shard_map(body, mesh=mesh, in_specs=in_specs, out_specs=out_specs, check_vma=False)
```

profile of v0, /device:TPU:1, one launch (start us, length us, event | category | flops | bytes accessed | tf_op | source)
XLA Modules:
  0.0 1158.5 jit_solution(15128348264181698341)
XLA Ops:
  11.2 10.7 gather_fusion
  21.9 9.4 copy.180
  32.3 18.4 %all-to-all-start = ((f32[32,2,8,256]{3,2,1,0:T(8,128)}), f32[32,2,8,256]{3,2,1,0:T(8,128)S(1)}, u32[]{:S(2)}, u32[]{:S(2)}) async-start(f32[32,2,8,256]{3,2,1,0:T(8,128)} %broadcast_multiply_fusion), calls=%async_computation | async-start | bytes 1048576 | tf_op jit(solution)/shard_map/all_to_all | solution.py:86
  51.2 31.6 %all-to-all-done = f32[32,2,8,256]{3,2,1,0:T(8,128)S(1)} async-done(((f32[32,2,8,256]{3,2,1,0:T(8,128)}), f32[32,2,8,256]{3,2,1,0:T(8,128)S(1)}, u32[]{:S(2)}, u32[]{:S(2)}) %all-to-all-start) | async-done | bytes 524320 | tf_op jit(solution)/shard_map/all_to_all | solution.py:86
  84.4 34.2 %all-gather.2.cloned.1.call-done = f32[6,2,128,256]{3,0,2,1:T(8,128)} async-done(((f32[6,2,8,256]{3,0,2,1:T(8,128)}), f32[6,2,128,256]{3,0,2,1:T(8,128)}) %all-gather.2.cloned.1.call-update) | async-done | bytes 1572880 | tf_op jit(solution)/shard_map/all_gather | solution.py:96
  138.3 133.8 %all-reduce.9.cloned.1.call-done = f32[2,256,256]{2,1,0:T(8,128)} async-done(((f32[2,256,256]{2,1,0:T(8,128)}), f32[2,256,256]{2,1,0:T(8,128)}) %all-reduce.9.cloned.1.call-update) | async-done | bytes 524304 | tf_op jit(solution)/shard_map/psum | solution.py:52
  287.0 281.3 %all-reduce.11.cloned.1.call-done = (f32[2,1,256,256]{3,2,1,0:T(8,128)}, f32[256,256]{1,0:T(8,128)}) async-done(((f32[2,1,256,256]{3,2,1,0:T(8,128)}, f32[256,256]{1,0:T(8,128)}), (f32[2,1,256,256]{3,2,1,0:T(8,128)}, f32[256,256]{1,0:T(8,128)})) %all-reduce.11.cloned.1.call-update) | async-done | bytes 786448 | tf_op jit(solution)/shard_map/psum | solution.py:112
  584.1 150.5 %all-reduce.13.cloned.1.call-done = (f32[256,256]{1,0:T(8,128)}, f32[2,256,256]{2,1,0:T(8,128)}) async-done(((f32[256,256]{1,0:T(8,128)}, f32[2,256,256]{2,1,0:T(8,128)}), (f32[256,256]{1,0:T(8,128)}, f32[2,256,256]{2,1,0:T(8,128)})) %all-reduce.13.cloned.1.call-update) | async-done | bytes 786448 | tf_op jit(solution)/shard_map/psum | solution.py:122
  763.1 64.6 %reduce-scatter.4.cloned.1.call-done = f32[8,3072]{1,0:T(8,128)} async-done(((f32[128,3072]{1,0:T(8,128)}), f32[8,3072]{1,0:T(8,128)}) %reduce-scatter.4.cloned.1.call-update) | async-done | bytes 98320
  830.7 14.2 %all-to-all-start.1 = ((f32[32,3,8,256]{3,2,1,0:T(8,128)}), f32[32,3,8,256]{3,2,1,0:T(8,128)S(1)}, u32[]{:S(2)}, u32[]{:S(2)}) async-start(f32[32,3,8,256]{3,2,1,0:T(8,128)} %copy.218), calls=%async_computation.1 | async-start | bytes 1572864 | tf_op jit(solution)/shard_map/all_to_all | solution.py:148
  845.0 38.9 %all-to-all-done.1 = f32[32,3,8,256]{3,2,1,0:T(8,128)S(1)} async-done(((f32[32,3,8,256]{3,2,1,0:T(8,128)}), f32[32,3,8,256]{3,2,1,0:T(8,128)S(1)}, u32[]{:S(2)}, u32[]{:S(2)}) %all-to-all-start.1) | async-done | bytes 786464 | tf_op jit(solution)/shard_map/all_to_all | solution.py:148
  884.1 240.9 %while.1 = (s32[]{:T(128)}, f32[32,3,8,512]{3,2,1,0:T(8,128)S(1)}, s32[32,4]{0,1:T(4,128)S(1)}, f32[32,3,8,256]{3,2,1,0:T(8,128)S(1)}, s32[]{:T(128)}, /*index=5*/s32[4]{0:T(128)S(1)}, s32[]{:T(128)}) while((s32[]{:T(128)}, f32[32,3,8,512]{3,2,1,0:T(8,128)S(1)}, s32[32,4]{0,1:T(4,128)S(1)}, f32[32,3,8,256]{3,2,1,0:T(8,128)S(1)}, s32[]{:T(128)}, ...), condition=%wide.while_cond, body=%wide.while_body.sunk | while | flops 6173 | bytes 123075 | solution.py:152
  884.8 3.2 and_reduce_fusion.2
  899.7 3.2 and_reduce_fusion.2
  907.2 3.2 and_reduce_fusion.2
  922.2 3.2 and_reduce_fusion.2
  937.5 3.2 and_reduce_fusion.2
  952.5 3.2 and_reduce_fusion.2
  967.4 3.2 and_reduce_fusion.2
  982.4 3.2 and_reduce_fusion.2
  997.4 3.2 and_reduce_fusion.2
  1012.7 3.2 and_reduce_fusion.2
  1027.7 3.2 and_reduce_fusion.2
  1125.9 25.0 %all_gather.7 = f32[2,128,512]{2,0,1:T(2,128)S(1)} all-gather(f32[2,8,512]{2,0,1:T(2,128)S(1)} %copy.219), channel_id=1, replica_groups=mesh['region'=32,'mode'=16] {'mode'}, dimensions={1}, use_global_device_ids=true | all-gather | bytes 557056 | tf_op jit(solution)/shard_map/all_gather | solution.py:157
  (264 shorter events, 294.8 us)
Async XLA Ops:
  31.3 19.4 %copy-start.8 = (s32[64,2]{0,1:T(2,128)S(1)}, s32[64,2]{0,1:T(2,128)}, u32[]{:S(2)}) copy-start(s32[64,2]{0,1:T(2,128)} %param.8) | copy-start | bytes 1540
  31.3 19.7 %copy-start.10 = (s32[32]{0:T(128)S(1)}, s32[32]{0:T(128)}, u32[]{:S(2)}) copy-start(s32[32]{0:T(128)} %param.9) | copy-start | bytes 388
  31.3 53.0 %copy-start.4 = (f32[2,1,256,256]{3,2,1,0:T(8,128)S(1)}, f32[2,1,256,256]{3,2,1,0:T(8,128)}, u32[]{:S(2)}) copy-start(f32[2,1,256,256]{3,2,1,0:T(8,128)} %param.6) | copy-start | bytes 1572868
  32.3 50.6 %all-to-all-start = ((f32[32,2,8,256]{3,2,1,0:T(8,128)}), f32[32,2,8,256]{3,2,1,0:T(8,128)S(1)}, u32[]{:S(2)}, u32[]{:S(2)}) async-start(f32[32,2,8,256]{3,2,1,0:T(8,128)} %broadcast_multiply_fusion), calls=%async_computation | async-start | bytes 1048576 | tf_op jit(solution)/shard_map/all_to_all | solution.py:86
  50.7 68.0 %all-gather.2.cloned.1.call-start = ((), (), s32[]{:S(2)}) async-start(), calls=%async_computation.3 | async-start | bytes 2228224 | tf_op jit(solution)/shard_map/all_gather | solution.py:96
  84.1 187.9 %all-reduce.9.cloned.1.call-start = ((), (), s32[]{:S(2)}) async-start(), calls=%async_computation.4 | async-start | bytes 1048576 | tf_op jit(solution)/shard_map/psum | solution.py:52
  135.5 136.6 %copy-start = (f32[2,256,256]{2,1,0:T(8,128)S(1)}, f32[2,256,256]{2,1,0:T(8,128)}, u32[]{:S(2)}) copy-start(f32[2,256,256]{2,1,0:T(8,128)} %param.5) | copy-start | bytes 1572868
  138.2 430.1 %all-reduce.11.cloned.1.call-start = ((), (), s32[]{:S(2)}) async-start(), calls=%async_computation.6 | async-start | bytes 1572864 | tf_op jit(solution)/shard_map/psum | solution.py:112
  272.0 3.2 copy-start.2
  286.1 283.2 %copy-start.5 = (f32[2,1,256,256]{3,2,1,0:T(8,128)S(1)}, f32[2,1,256,256]{3,2,1,0:T(8,128)}, u32[]{:S(2)}) copy-start(f32[2,1,256,256]{3,2,1,0:T(8,128)} %param.6) | copy-start | bytes 1572868
  286.9 447.7 %all-reduce.13.cloned.1.call-start = ((), (), s32[]{:S(2)}) async-start(), calls=%async_computation.7 | async-start | bytes 1572864 | tf_op jit(solution)/shard_map/psum | solution.py:122
  570.4 6.0 copy-start.3
  584.0 243.7 %reduce-scatter.4.cloned.1.call-start = ((), (), s32[]{:S(2)}) async-start(), calls=%async_computation.5 | async-start | bytes 1671168
  734.6 3.2 copy-start.1
  757.8 0.9 copy-start.6
  829.3 15.6 %copy-start.9 = (s32[3]{0:T(128)S(1)}, s32[3]{0:T(128)}, u32[]{:S(2)}) copy-start(s32[3]{0:T(128)} %constant.101.clone.1) | copy-start | bytes 40
  830.7 53.4 %copy-start.7 = (s32[4]{0:T(128)S(1)}, s32[4]{0:T(128)}, u32[]{:S(2)}) copy-start(s32[4]{0:T(128)} %constant.635) | copy-start | bytes 52
  830.7 53.2 %all-to-all-start.1 = ((f32[32,3,8,256]{3,2,1,0:T(8,128)}), f32[32,3,8,256]{3,2,1,0:T(8,128)S(1)}, u32[]{:S(2)}, u32[]{:S(2)}) async-start(f32[32,3,8,256]{3,2,1,0:T(8,128)} %copy.218), calls=%async_computation.1 | async-start | bytes 1572864 | tf_op jit(solution)/shard_map/all_to_all | solution.py:148
Sparse Core Ops, SparseCore 0:
  84.2 34.3 all-gather.1
  138.3 133.6 all-reduce.8
  287.0 281.1 all-reduce.10
  584.1 150.4 all-reduce.12
  758.0 69.6 reduce-scatter.3
where the time goes:
time: 1180 us; the launch traced here: 1160 us
  waiting for transfers between devices  735 us (62%)
  other arithmetic  177 us (15%)
  local copies, waits for them, and re-layouts  119 us (10%)
  matrix products  54.6 us (5%)
  starting transfers between devices  33 us (3%)
  blocking collectives  25 us (2%)
  between operations  14.6 us (1%)
    psum x1, waiting for transfers between devices, body(): gradient, power_total = lax.psum((gradient, object_power), 'region')  281 us
    scatter x64, other arithmetic  166 us
    psum x1, waiting for transfers between devices, body(): power_modes = lax.psum(mode_power, 'mode')  151 us
    psum x1, waiting for transfers between devices, wave_change(): summed = lax.psum(local_sum, 'mode')  134 us
    scatter x96, local copies, waits for them, and re-layouts  73.8 us
    unnamed x6, waiting for transfers between devices  64.7 us
    all_to_all x1, waiting for transfers between devices, body(): lax.all_to_all(outgoing_update, 'region', split_axis=0, concat_axis=0, ti...  38.9 us
    all_gather x1, waiting for transfers between devices, body(): assembled = lax.all_gather(chosen, 'mode', axis=2, tiled=True)  34.2 us
  transfers between devices with their start and end apart: 7, of which 7 were waited for; matrix products, arithmetic and copies ran while one was open for 0% of the time, Pallas kernels for 0%

commit v1 on v0

v1 whole, which is shorter than its diff:
```python
import functools
import math

import jax
import jax.numpy as jnp
import numpy as np
from jax import lax
from jax.experimental import pallas as pl
from jax.experimental.pallas import tpu as pltpu
from jax.sharding import PartitionSpec as P

N = 256
BAND = 128
WIDTH = 512
FRAMES = 64
F_DEV = 2
REGIONS = 32
MODES = 16
Z = 16
Y = 4
SHARE = BAND // MODES
f32 = jnp.float32
bf16 = jnp.bfloat16

VMEM = pl.BlockSpec(memory_space=pltpu.VMEM)
SMEM = pl.BlockSpec(memory_space=pltpu.SMEM)
DMA = pltpu.SemaphoreType.DMA

NEAR = ((2, 1), (2, 0), (1, 1), (3, 1), (1, 0), (3, 0), (0, 1), (0, 0))
OTHERS = len(NEAR) - 1


def send(src, dst, send_sem, recv_sem, axis, index):
    copy = pltpu.make_async_remote_copy(
        src_ref=src,
        dst_ref=dst,
        send_sem=send_sem,
        recv_sem=recv_sem,
        device_id={axis: index},
        device_id_type=pl.DeviceIdType.MESH,
    )
    copy.start()
    return copy


def greet(axis, peers):
    barrier = pltpu.get_barrier_semaphore()
    for peer in peers:
        pl.semaphore_signal(
            barrier, inc=1, device_id={axis: peer}, device_id_type=pl.DeviceIdType.MESH
        )
    pl.semaphore_wait(barrier, len(peers))


class ModeGroup:
    def __init__(self):
        self.me = lax.axis_index("mode")
        self.y = self.me // 4
        self.x = (self.me // 2) % 2
        self.core = self.me % 2
        self.twin = self.me + 1 - 2 * self.core

    def chip(self, dy, dx):
        return ((self.y + dy) % Y) * 2 + (self.x + dx) % 2

    def chip_before(self, dy, dx):
        return ((self.y + Y - dy) % Y) * 2 + (self.x + 2 - dx) % 2

    def peers(self):
        return [2 * self.chip(dy, dx) + self.core for dy, dx in NEAR[:OTHERS]] + [self.twin]


def mode_scatter(group, x_ref, twin_buf, peer_buf, sems):
    twin_send, twin_recv, peer_send, peer_recv = sems
    twin_copies = []
    for i, (dy, dx) in enumerate(NEAR):
        block = 2 * group.chip(dy, dx) + 1 - group.core
        twin_copies.append(
            send(x_ref.at[:, block], twin_buf.at[i], twin_send.at[i], twin_recv.at[i], "mode", group.twin)
        )
    peer_copies = []
    for i, (dy, dx) in enumerate(NEAR):
        target = 2 * group.chip(dy, dx) + group.core
        twin_copies[i].wait_recv()
        twin_buf[i] = twin_buf[i] + x_ref[:, target]
        if i < OTHERS:
            peer_copies.append(
                send(twin_buf.at[i], peer_buf.at[i], peer_send.at[i], peer_recv.at[i], "mode", target)
            )
    total = twin_buf[OTHERS]
    for i in reversed(range(OTHERS)):
        peer_copies[i].wait_recv()
        total = total + peer_buf[i]
    return total, twin_copies + peer_copies


def mode_gather(group, out_ref, sems):
    twin_send, twin_recv, peer_send, peer_recv = sems
    mine = out_ref.at[:, group.me]
    peer_copies = []
    for i, (dy, dx) in enumerate(NEAR[:OTHERS]):
        target = 2 * group.chip(dy, dx) + group.core
        peer_copies.append(send(mine, mine, peer_send.at[i], peer_recv.at[i], "mode", target))
    twin_copies = [
        send(mine, mine, twin_send.at[OTHERS], twin_recv.at[OTHERS], "mode", group.twin)
    ]
    for i in reversed(range(OTHERS)):
        dy, dx = NEAR[i]
        block = out_ref.at[:, 2 * group.chip_before(dy, dx) + group.core]
        peer_copies[i].wait_recv()
        twin_copies.append(send(block, block, twin_send.at[i], twin_recv.at[i], "mode", group.twin))
    for copy in twin_copies:
        copy.wait_recv()
    return twin_copies + peer_copies


class RegionGroup:
    def __init__(self):
        self.me = lax.axis_index("region")
        self.x = self.me // Z
        self.z = self.me % Z
        self.right = self.x * Z + (self.z + 1) % Z
        self.left = self.x * Z + (self.z + Z - 1) % Z
        self.partner = (1 - self.x) * Z + self.z

    def block(self, half, z):
        side = self.x if half == 1 else 1 - self.x
        return side * Z + z % Z

    def peers(self):
        return [self.right, self.left, self.partner]


RIGHT_STEPS = Z // 2
LEFT_STEPS = Z - 1 - RIGHT_STEPS


def region_scatter(group, x_ref, right_buf, left_buf, side_buf, sems):
    right_send, right_recv, left_send, left_recv, side_send, side_recv = sems
    rights = {}
    lefts = {}

    def go_right(half, step, src):
        rights[half, step] = send(
            src, right_buf.at[half, step], right_send.at[half, step], right_recv.at[half, step],
            "region", group.right,
        )

    def go_left(half, step, src):
        lefts[half, step] = send(
            src, left_buf.at[half, step], left_send.at[half, step], left_recv.at[half, step],
            "region", group.left,
        )

    for half in (0, 1):
        go_right(half, 0, x_ref.at[:, group.block(half, group.z + RIGHT_STEPS)])
        go_left(half, 0, x_ref.at[:, group.block(half, group.z + Z - LEFT_STEPS)])
    for step in range(1, RIGHT_STEPS):
        for half in (0, 1):
            rights[half, step - 1].wait_recv()
            own = x_ref[:, group.block(half, group.z + RIGHT_STEPS - step)]
            right_buf[half, step - 1] = right_buf[half, step - 1] + own
            go_right(half, step, right_buf.at[half, step - 1])
            if step < LEFT_STEPS:
                lefts[half, step - 1].wait_recv()
                own = x_ref[:, group.block(half, group.z + Z - LEFT_STEPS + step)]
                left_buf[half, step - 1] = left_buf[half, step - 1] + own
                go_left(half, step, left_buf.at[half, step - 1])
    totals = []
    side = None
    for half in (0, 1):
        lefts[half, LEFT_STEPS - 1].wait_recv()
        own = x_ref[:, group.block(half, group.z)] + left_buf[half, LEFT_STEPS - 1]
        rights[half, RIGHT_STEPS - 1].wait_recv()
        total = own + right_buf[half, RIGHT_STEPS - 1]
        if half == 0:
            right_buf[half, RIGHT_STEPS - 1] = total
            side = send(
                right_buf.at[half, RIGHT_STEPS - 1], side_buf, side_send.at[0], side_recv.at[0],
                "region", group.partner,
            )
        else:
            totals.append(total)
    side.wait_recv()
    return totals[0] + side_buf[...], list(rights.values()) + list(lefts.values()) + [side]


def region_gather(group, src_ref, out_ref, sems):
    right_send, right_recv, left_send, left_recv, side_send, side_recv = sems
    rights = {}
    lefts = {}
    mine = out_ref.at[:, group.me]
    side = send(src_ref, mine, side_send.at[0], side_recv.at[0], "region", group.partner)
    for step in range(RIGHT_STEPS):
        for half in (1, 0):
            if step == 0 and half == 0:
                side.wait_recv()
            if step > 0:
                rights[half, step - 1].wait_recv()
            block = out_ref.at[:, group.block(half, group.z + Z - step)]
            source = src_ref if (step == 0 and half == 1) else block
            rights[half, step] = send(
                source, block, right_send.at[half, step], right_recv.at[half, step],
                "region", group.right,
            )
            if step < LEFT_STEPS:
                if step > 0:
                    lefts[half, step - 1].wait_recv()
                block = out_ref.at[:, group.block(half, group.z + step)]
                source = src_ref if (step == 0 and half == 1) else block
                lefts[half, step] = send(
                    source, block, left_send.at[half, step], left_recv.at[half, step],
                    "region", group.left,
                )
    for half in (1, 0):
        lefts[half, LEFT_STEPS - 1].wait_recv()
        rights[half, RIGHT_STEPS - 1].wait_recv()
    return list(rights.values()) + list(lefts.values()) + [side]


def finish(copies):
    for copy in copies:
        copy.wait_send()


MODE_SEMS = [DMA((OTHERS + 1,)), DMA((OTHERS + 1,)), DMA((OTHERS,)), DMA((OTHERS,))]
REGION_SEMS = [
    DMA((2, RIGHT_STEPS)), DMA((2, RIGHT_STEPS)), DMA((2, LEFT_STEPS)), DMA((2, LEFT_STEPS)),
    DMA((1,)), DMA((1,)),
]


def params(collective_id=None):
    if collective_id is None:
        return pltpu.CompilerParams(vmem_limit_bytes=56 * 2**20)
    return pltpu.CompilerParams(
        collective_id=collective_id, has_side_effects=True, vmem_limit_bytes=56 * 2**20
    )


def call(kernel, name, outs, n_smem, args, scratch=(), collective_id=None):
    return pl.pallas_call(
        kernel,
        name=name,
        out_shape=[jax.ShapeDtypeStruct(shape, f32) for shape in outs],
        in_specs=[SMEM] * n_smem + [VMEM] * (len(args) - n_smem),
        out_specs=[VMEM] * len(outs),
        scratch_shapes=list(scratch),
        compiler_params=params(collective_id),
    )(*args)


def gather_bands_kernel(object_ref, out_ref, *sems):
    group = RegionGroup()
    share = lax.axis_index("mode")
    greet("region", group.peers())
    copies = region_gather(group, object_ref.at[:, share], out_ref, sems)
    out_ref[:, group.me] = object_ref[:, share]
    finish(copies)


def gather_mode_kernel(x_ref, out_ref, *sems):
    group = ModeGroup()
    greet("mode", group.peers())
    out_ref[:, group.me] = x_ref[...]
    finish(mode_gather(group, out_ref, sems))


def reduce_mode_kernel(x_ref, out_ref, twin_buf, peer_buf, *sems):
    group = ModeGroup()
    greet("mode", group.peers())
    total, copies = mode_scatter(group, x_ref, twin_buf, peer_buf, sems[:4])
    out_ref[:, group.me] = total
    copies = copies + mode_gather(group, out_ref, sems[4:])
    finish(copies)


def scatter_mode_kernel(x_ref, out_ref, twin_buf, peer_buf, *sems):
    group = ModeGroup()
    greet("mode", group.peers())
    total, copies = mode_scatter(group, x_ref, twin_buf, peer_buf, sems)
    out_ref[...] = total
    finish(copies)


def refine_kernel(x_ref, probe_ref, out_ref, right_buf, left_buf, side_buf, *sems):
    group = RegionGroup()
    greet("region", group.peers())
    total, copies = region_scatter(group, x_ref, right_buf, left_buf, side_buf, sems[:6])
    scale = total[2:3] + 1.0
    out_ref[:, group.me] = probe_ref[:, group.me] + total[0:2] / scale
    copies = copies + region_gather(group, out_ref.at[:, group.me], out_ref, sems[6:])
    finish(copies)


def scatter_region_kernel(x_ref, out_ref, right_buf, left_buf, side_buf, *sems):
    group = RegionGroup()
    greet("region", group.peers())
    total, copies = region_scatter(group, x_ref, right_buf, left_buf, side_buf, sems)
    out_ref[...] = total
    finish(copies)


def mode_buffers(a, rows, width):
    return [pltpu.VMEM((OTHERS + 1, a, rows, width), f32), pltpu.VMEM((OTHERS, a, rows, width), f32)]


def region_buffers(a, rows, width):
    return [
        pltpu.VMEM((2, RIGHT_STEPS, a, rows, width), f32),
        pltpu.VMEM((2, LEFT_STEPS, a, rows, width), f32),
        pltpu.VMEM((a, rows, width), f32),
    ]


def frame_place(scan_ref, owner_ref, frame):
    number = lax.axis_index("region") * F_DEV + frame
    first = scan_ref[number, 0]
    anchor = first // BAND
    homes = [owner_ref[anchor + k] for k in range(3)]
    return homes, first - anchor * BAND, anchor % 2, scan_ref[number, 1]


def row_numbers(width):
    rows = lax.broadcasted_iota(jnp.int32, (SHARE, width), 0)
    return rows + lax.axis_index("mode") * SHARE


def select_kernel(scan_ref, owner_ref, bands_ref, out_ref):
    numbers = row_numbers(WIDTH)
    for frame in range(F_DEV):
        homes, lead, odd, column = frame_place(scan_ref, owner_ref, frame)
        back = (WIDTH - column) % WIDTH
        for plane in range(2):
            outer = jnp.where(numbers >= lead, bands_ref[plane, homes[0]], bands_ref[plane, homes[2]])
            inner = bands_ref[plane, homes[1]]
            outer = pltpu.roll(outer, back, 1)[:, :N]
            inner = pltpu.roll(inner, back, 1)[:, :N]
            out_ref[(frame * 2 + plane) * 2 + odd] = outer
            out_ref[(frame * 2 + plane) * 2 + 1 - odd] = inner


def place_kernel(scan_ref, owner_ref, terms_ref, out_ref):
    out_ref[...] = jnp.zeros(out_ref.shape, f32)
    numbers = row_numbers(WIDTH)
    blank = jnp.zeros((SHARE, WIDTH - N), f32)
    for frame in range(F_DEV):
        homes, lead, odd, column = frame_place(scan_ref, owner_ref, frame)
        for plane in range(2):
            outer = terms_ref[(frame * 2 + plane) * 2 + odd]
            inner = terms_ref[(frame * 2 + plane) * 2 + 1 - odd]
            outer = pltpu.roll(jnp.concatenate([outer, blank], axis=1), column, 1)
            inner = pltpu.roll(jnp.concatenate([inner, blank], axis=1), column, 1)
            out_ref[plane, homes[0]] = jnp.where(numbers >= lead, outer, 0.0)
            out_ref[plane, homes[1]] = inner
            out_ref[plane, homes[2]] = jnp.where(numbers >= lead, 0.0, outer)


def update_kernel(scan_ref, owner_ref, terms_ref, object_ref, power_ref, out_ref, tall, density):
    region = lax.axis_index("region")
    share = lax.axis_index("mode")
    own_band = lax.fori_loop(
        0, REGIONS, lambda b, found: found + jnp.where(owner_ref[b] == region, b, 0), 0
    )
    tall[0:BAND, :] = jnp.zeros((BAND, N), f32)
    tall[BAND:BAND + N, :] = power_ref[...]
    tall[BAND + N:, :] = jnp.zeros((BAND + SHARE, N), f32)
    density[...] = jnp.zeros(density.shape, f32)
    blank = jnp.zeros((SHARE, WIDTH - N), f32)

    @pl.loop(0, FRAMES)
    def _(number):
        first = scan_ref[number, 0]
        offset = own_band - first // BAND

        @pl.when(jnp.logical_and(offset >= 0, offset <= 2))
        def _():
            start = BAND + own_band * BAND - first + share * SHARE
            base = pl.multiple_of(start // 8 * 8, 8)
            rows = tall[pl.ds(base, 2 * SHARE), :]
            rows = pltpu.roll(rows, (2 * SHARE - start % 8) % (2 * SHARE), 0)[:SHARE]
            wide = jnp.concatenate([rows, blank], axis=1)
            density[...] = density[...] + pltpu.roll(wide, scan_ref[number, 1], 1)

    scale = density[...] + 1.0
    for plane in range(2):
        out_ref[plane] = object_ref[plane, share] + terms_ref[plane] / scale


def split(x):
    high = x.astype(bf16)
    low = (x - high.astype(f32)).astype(bf16)
    return high, low


def transform(real, imag, tables, sign):
    ch, cl, sh, sl = tables
    cosine = jnp.concatenate([ch, ch, cl], axis=1)
    sine = jnp.concatenate([sh, sh, sl], axis=1)
    minus = -sine
    if sign < 0:
        left_real = jnp.concatenate([cosine, sine], axis=1)
        left_imag = jnp.concatenate([minus, cosine], axis=1)
    else:
        left_real = jnp.concatenate([cosine, minus], axis=1)
        left_imag = jnp.concatenate([sine, cosine], axis=1)
    rh, rl = split(real)
    ih, il = split(imag)
    stacked = jnp.concatenate([rh, rl, rh, ih, il, ih], axis=0)
    mid_real = jnp.dot(left_real, stacked, preferred_element_type=f32)
    mid_imag = jnp.dot(left_imag, stacked, preferred_element_type=f32)
    rh, rl = split(mid_real)
    ih, il = split(mid_imag)
    beside = jnp.concatenate([rh, rl, rh, ih, il, ih], axis=1)
    cosine = jnp.concatenate([ch, ch, cl], axis=0)
    sine = jnp.concatenate([sh, sh, sl], axis=0)
    minus = -sine
    if sign < 0:
        right_real = jnp.concatenate([cosine, sine], axis=0)
        right_imag = jnp.concatenate([minus, cosine], axis=0)
    else:
        right_real = jnp.concatenate([cosine, minus], axis=0)
        right_imag = jnp.concatenate([sine, cosine], axis=0)
    return (
        jnp.dot(beside, right_real, preferred_element_type=f32),
        jnp.dot(beside, right_imag, preferred_element_type=f32),
    )


def load_tables(tables_ref):
    return tuple(tables_ref[i] for i in range(4))


def forward_waves(windows_ref, probe_ref, tables, wave_ref, out_ref):
    for frame in range(F_DEV):
        wr, wi = windows_ref[frame, 0], windows_ref[frame, 1]
        pr, pi = probe_ref[0], probe_ref[1]
        real, imag = transform(pr * wr - pi * wi, pr * wi + pi * wr, tables, -1)
        wave_ref[frame, 0] = real
        wave_ref[frame, 1] = imag
        out_ref[frame] = real * real + imag * imag


def first_wave_kernel(scan_ref, turned_ref, probe_ref, tables_ref, windows_ref, wave_ref, out_ref):
    region = lax.axis_index("region")
    for frame in range(F_DEV):
        back = (N - scan_ref[region * F_DEV + frame, 0] % N) % N
        for plane in range(2):
            windows_ref[frame, plane] = pltpu.roll(turned_ref[frame, plane], back, 0)
    forward_waves(windows_ref, probe_ref, load_tables(tables_ref), wave_ref, out_ref)


def second_wave_kernel(windows_ref, probe_ref, tables_ref, wave_ref, out_ref):
    forward_waves(windows_ref, probe_ref, load_tables(tables_ref), wave_ref, out_ref)
    out_ref[F_DEV] = probe_ref[0] * probe_ref[0] + probe_ref[1] * probe_ref[1]


def change_of(frame, wave_ref, intensity_ref, measured_ref, tables):
    factor = jnp.sqrt(measured_ref[frame]) / jnp.sqrt(intensity_ref[frame] + 0.1) - 1.0
    return transform(wave_ref[frame, 0] * factor, wave_ref[frame, 1] * factor, tables, 1)


def gradient_kernel(wave_ref, intensity_ref, measured_ref, windows_ref, tables_ref, out_ref):
    tables = load_tables(tables_ref)
    for frame in range(F_DEV):
        cr, ci = change_of(frame, wave_ref, intensity_ref, measured_ref, tables)
        wr, wi = windows_ref[frame, 0], windows_ref[frame, 1]
        parts = (wr * cr + wi * ci, wr * ci - wi * cr, wr * wr + wi * wi)
        for k, part in enumerate(parts):
            out_ref[k] = part if frame == 0 else out_ref[k] + part


def terms_kernel(scan_ref, wave_ref, intensity_ref, measured_ref, probe_ref, tables_ref, out_ref):
    region = lax.axis_index("region")
    tables = load_tables(tables_ref)
    for frame in range(F_DEV):
        cr, ci = change_of(frame, wave_ref, intensity_ref, measured_ref, tables)
        pr, pi = probe_ref[0], probe_ref[1]
        turn = scan_ref[region * F_DEV + frame, 0] % N
        out_ref[frame, 0] = pltpu.roll(pr * cr + pi * ci, turn, 0)
        out_ref[frame, 1] = pltpu.roll(pr * ci - pi * cr, turn, 0)


def table_array():
    product = np.arange(N)[:, None] * np.arange(N)[None, :] % N
    angles = product * (2.0 * math.pi / N)
    pieces = []
    for values in (np.cos(angles) / 16.0, np.sin(angles) / 16.0):
        high = values.astype(bf16)
        pieces += [high, (values - high.astype(np.float64)).astype(bf16)]
    return np.stack(pieces)


def body(measured, probe_modes, object_bands, scan_offsets, band_owner):
    tables = jnp.asarray(table_array())
    probe = probe_modes[:, 0]
    shares = object_bands.reshape(2, MODES, SHARE, WIDTH)
    image_shape = (2, REGIONS, SHARE, WIDTH)
    (bands,) = call(gather_bands_kernel, "gather_bands", [image_shape], 0, [shares], REGION_SEMS, 1)
    (chosen,) = call(
        select_kernel, "select", [(8, SHARE, N)], 2, [scan_offsets, band_owner, bands]
    )
    (turned,) = call(gather_mode_kernel, "gather_windows", [(8, MODES, SHARE, N)], 0, [chosen], MODE_SEMS, 2)
    frame_shape = (F_DEV, 2, N, N)
    windows, wave, intensity = call(
        first_wave_kernel, "first_wave", [frame_shape, frame_shape, (F_DEV, N, N)], 1,
        [scan_offsets, turned.reshape(frame_shape), probe, tables],
    )
    (summed,) = call(
        reduce_mode_kernel, "sum_intensity", [(2, MODES, 16, N)], 0,
        [intensity.reshape(2, MODES, 16, N)], mode_buffers(2, 16, N) + MODE_SEMS * 2, 3,
    )
    (gradient,) = call(
        gradient_kernel, "gradient", [(3, N, N)], 0,
        [wave, summed.reshape(F_DEV, N, N), measured, windows, tables],
    )
    (probe,) = call(
        refine_kernel, "refine", [(2, REGIONS, 8, N)], 0,
        [gradient.reshape(3, REGIONS, 8, N), probe.reshape(2, REGIONS, 8, N)],
        region_buffers(3, 8, N) + REGION_SEMS * 2, 4,
    )
    probe = probe.reshape(2, N, N)
    wave, intensity = call(
        second_wave_kernel, "second_wave", [frame_shape, (F_DEV + 1, N, N)], 0,
        [windows, probe, tables],
    )
    (summed,) = call(
        reduce_mode_kernel, "sum_second", [(3, MODES, 16, N)], 0,
        [intensity.reshape(3, MODES, 16, N)], mode_buffers(3, 16, N) + MODE_SEMS * 2, 5,
    )
    summed = summed.reshape(3, N, N)
    (terms,) = call(
        terms_kernel, "terms", [frame_shape], 1,
        [scan_offsets, wave, summed, measured, probe, tables],
    )
    (terms,) = call(
        scatter_mode_kernel, "scatter_terms", [(8, SHARE, N)], 0,
        [terms.reshape(8, MODES, SHARE, N)], mode_buffers(8, SHARE, N) + MODE_SEMS, 6,
    )
    (placed,) = call(
        place_kernel, "place", [image_shape], 2, [scan_offsets, band_owner, terms]
    )
    (update,) = call(
        scatter_region_kernel, "scatter_update", [(2, SHARE, WIDTH)], 0, [placed],
        region_buffers(2, SHARE, WIDTH) + REGION_SEMS, 7,
    )
    (rows,) = call(
        update_kernel, "update", [(2, SHARE, WIDTH)], 2,
        [scan_offsets, band_owner, update, shares, summed[F_DEV]],
        [pltpu.VMEM((2 * BAND + N + SHARE, N), f32), pltpu.VMEM((SHARE, WIDTH), f32)],
    )
    (object_out,) = call(
        gather_mode_kernel, "gather_rows", [(2, MODES, SHARE, WIDTH)], 0, [rows], MODE_SEMS, 8
    )
    return probe[:, None], object_out.reshape(2, BAND, WIDTH)


def solution(mesh):
    in_specs = (
        P("region", None, None),
        P(None, "mode", None, None),
        P(None, "region", None),
        P(),
        P(),
    )
    out_specs = (P(None, "mode", None, None), P(None, "region", None))
    return jax.shard_map(body, mesh=mesh, in_specs=in_specs, out_specs=out_specs, check_vma=False)
```

time: 1180 us -> 250 us (0.21); the launches traced: 1160 us -> 249 us
  waiting for transfers between devices: 735 us -> 0 us
  Pallas kernels: 0 us -> 244 us
  other arithmetic: 177 us -> 0 us
  local copies, waits for them, and re-layouts: 119 us -> 5.07 us
  matrix products: 54.6 us -> 0 us
  starting transfers between devices: 33 us -> 0 us
  blocking collectives: 25 us -> 0 us
  between operations: 14.6 us -> 0.71 us
    psum x3 -> x0, waiting for transfers between devices: 566 us -> none  [the longest x1 281 us: body(): gradient, power_total = lax.psum((gradient, object_power), 'region')]
    pallas_call x0 -> x15, Pallas kernels: none -> 244 us  [call(): pl.pallas_call(kernel, name=name, out_shape=[jax.ShapeDtypeStruct(shape,...]
    scatter x65 -> x0, other arithmetic: 166 us -> none
    scatter x96 -> x0, local copies, waits for them, and re-layouts: 73.8 us -> none
    all_to_all x2 -> x0, waiting for transfers between devices: 70.5 us -> none  [the longest x1 38.9 us: body(): lax.all_to_all(outgoing_update, 'region', split_axis=0, concat_axis=0, ti...]
    unnamed x6 -> x0, waiting for transfers between devices: 64.7 us -> none
    dot_general x26 -> x0, matrix products: 54.6 us -> none  [the longest x12 26.5 us: left_product(): return jnp.einsum('jk,...kl->...jl', matrix, planes, precision=highest)]
    all_gather x1 -> x0, waiting for transfers between devices: 34.2 us -> none  [body(): assembled = lax.all_gather(chosen, 'mode', axis=2, tiled=True)]
  transfers between devices with their start and end apart: 7 -> 0, of which waited for: 7 -> 0; matrix products, arithmetic and copies ran while one was open for 0% -> 0% of each run, Pallas kernels for 0% -> 0%
where the time goes in v1:
time: 250 us; the launch traced here: 249 us
  Pallas kernels  244 us (98%)
  local copies, waits for them, and re-layouts  5.07 us (2%)
    pallas_call x15, Pallas kernels, call(): pl.pallas_call(kernel, name=name, out_shape=[jax.ShapeDtypeStruct(shape,...  244 us

profile of v1, /device:TPU:1, one launch (start us, length us, event | category | flops | bytes accessed | tf_op | source)
XLA Modules:
  0.0 249.4 jit_solution(6323386202528080306)
XLA Ops:
  0.6 1.4 copy.9.scan_ref
  2.0 36.4 %gather_bands.1.bands_ref = f32[2,32,8,512]{3,2,1,0:T(8,128)} custom-call(f32[2,16,8,512]{3,2,1,0:T(8,128)} %bitcast.23), custom_call_target="tpu_custom_call" | custom-call | tf_op jit(solution)/shard_map/gather_bands/pallas_call | solution.py:242
  38.4 2.0 select.1.x_ref
  40.4 21.8 %gather_windows.1 = f32[8,16,8,256]{3,2,1,0:T(8,128)} custom-call(f32[8,8,256]{2,1,0:T(8,128)} %select.1.x_ref), custom_call_target="tpu_custom_call" | custom-call | tf_op jit(solution)/shard_map/gather_windows/pallas_call | solution.py:242
  62.2 5.0 %first_wave.1 = (f32[2,2,256,256]{3,2,1,0:T(8,128)}, f32[2,2,256,256]{3,2,1,0:T(8,128)}, f32[2,256,256]{2,1,0:T(8,128)}) custom-call(s32[64,2]{1,0:T(8,128)} %copy.9.scan_ref, f32[2,2,256,256]{3,2,1,0:T(8,128)} %bitcast.21, f32[2,256,256]{2,1,0:T(8,128)} %bitcast.26, bf16[4,256,256]{2,1,0:T(8,128)(2,1)} %constant.2.clone.tables_ref), custom_call_target="tpu_custom_call" | custom-call | tf_op jit(solution)/shard_map/first_wave/pallas_call | solution.py:242
  67.2 17.7 %sum_intensity.1 = f32[2,16,16,256]{3,2,1,0:T(8,128)} custom-call(f32[2,16,16,256]{3,2,1,0:T(8,128)} %bitcast.31), custom_call_target="tpu_custom_call" | custom-call | tf_op jit(solution)/shard_map/sum_intensity/pallas_call | solution.py:242
  84.9 5.1 %gradient.1 = f32[3,256,256]{2,1,0:T(8,128)} custom-call(f32[2,2,256,256]{3,2,1,0:T(8,128)} %get-tuple-element.7.wave_ref, f32[2,256,256]{2,1,0:T(8,128)} %bitcast.25, f32[2,256,256]{2,1,0:T(8,128)} %measured_ref.3, f32[2,2,256,256]{3,2,1,0:T(8,128)} %get-tuple-element.9.windows_ref, bf16[4,256,256]{2,1,0:T(8,128)(2,1)} %constant.2.clone.tables_ref), custom_call_target="tpu_custom_call" | custom-call | tf_op jit(solution)/shard_map/gradient/pallas_call | solution.py:242
  90.0 46.9 %refine.1 = f32[2,32,8,256]{3,2,1,0:T(8,128)} custom-call(f32[3,32,8,256]{3,2,1,0:T(8,128)} %bitcast.22, f32[2,32,8,256]{3,2,1,0:T(8,128)} %bitcast.27), custom_call_target="tpu_custom_call" | custom-call | tf_op jit(solution)/shard_map/refine/pallas_call | solution.py:242
  136.9 4.7 %second_wave.1 = (f32[2,2,256,256]{3,2,1,0:T(8,128)}, f32[3,256,256]{2,1,0:T(8,128)}) custom-call(f32[2,2,256,256]{3,2,1,0:T(8,128)} %get-tuple-element.9.windows_ref, f32[2,256,256]{2,1,0:T(8,128)} %bitcast.16, bf16[4,256,256]{2,1,0:T(8,128)(2,1)} %constant.2.clone.tables_ref), custom_call_target="tpu_custom_call" | custom-call | tf_op jit(solution)/shard_map/second_wave/pallas_call | solution.py:242
  141.7 34.6 %sum_second.1 = f32[3,16,16,256]{3,2,1,0:T(8,128)} custom-call(f32[3,16,16,256]{3,2,1,0:T(8,128)} %bitcast.30), custom_call_target="tpu_custom_call" | custom-call | tf_op jit(solution)/shard_map/sum_second/pallas_call | solution.py:242
  176.3 5.3 %terms.1 = f32[2,2,256,256]{3,2,1,0:T(8,128)} custom-call(s32[64,2]{1,0:T(8,128)} %copy.9.scan_ref, f32[2,2,256,256]{3,2,1,0:T(8,128)} %get-tuple-element.10.wave_ref, f32[3,256,256]{2,1,0:T(8,128)} %bitcast.19, f32[2,256,256]{2,1,0:T(8,128)} %measured_ref.3, f32[2,256,256]{2,1,0:T(8,128)} %bitcast.17, bf16[4,256,256]{2,1,0:T(8,128)(2,1)} %constant.2.clone.tables_ref), custom_call_target="tpu_custom_call" | custom-call | tf_op jit(solution)/shard_map/terms/pallas_call | solution.py:242
  181.6 14.5 %scatter_terms.1.terms_ref = f32[8,8,256]{2,1,0:T(8,128)} custom-call(f32[8,16,8,256]{3,2,1,0:T(8,128)} %bitcast.20), custom_call_target="tpu_custom_call" | custom-call | tf_op jit(solution)/shard_map/scatter_terms/pallas_call | solution.py:242
  196.2 2.3 place.1.x_ref
  198.4 25.9 %scatter_update.1.terms_ref = f32[2,8,512]{2,1,0:T(8,128)} custom-call(f32[2,32,8,512]{3,2,1,0:T(8,128)} %place.1.x_ref), custom_call_target="tpu_custom_call" | custom-call | tf_op jit(solution)/shard_map/scatter_update/pallas_call | solution.py:242
  224.4 1.7 slice.4
  226.0 0.0 copy-start
  226.0 3.8 %update.1.x_ref = f32[2,8,512]{2,1,0:T(8,128)} custom-call(s32[64,2]{1,0:T(8,128)} %copy.9.scan_ref, s32[32]{0:T(128)} %owner_ref.5, f32[2,8,512]{2,1,0:T(8,128)} %scatter_update.1.terms_ref, f32[2,16,8,512]{3,2,1,0:T(8,128)} %bitcast.24, f32[256,256]{1,0:T(8,128)} %bitcast.29), custom_call_target="tpu_custom_call" | custom-call | tf_op jit(solution)/shard_map/update/pallas_call | solution.py:242
  229.9 17.5 %gather_rows.1 = f32[2,16,8,512]{3,2,1,0:T(8,128)} custom-call(f32[2,8,512]{2,1,0:T(8,128)} %update.1.x_ref), custom_call_target="tpu_custom_call" | custom-call | tf_op jit(solution)/shard_map/gather_rows/pallas_call | solution.py:242
  247.3 0.0 copy-done
  247.3 0.0 copy-start.1
  247.3 0.8 copy.16
  248.1 0.4 copy-done.1
  248.6 0.8 copy.17
Async XLA Ops:
  226.0 21.3 %copy-start = (f32[2,32,8,256]{3,2,1,0:T(8,128)S(1)}, f32[2,32,8,256]{3,2,1,0:T(8,128)}, u32[]{:S(2)}) copy-start(f32[2,32,8,256]{3,2,1,0:T(8,128)} %refine.1) | copy-start | bytes 1572868
  247.3 1.2 copy-start.1

commit v2 on v0

v2 whole, which is shorter than its diff:
```python
import functools
import math

import jax
import jax.numpy as jnp
import numpy as np
from jax import lax
from jax.experimental import pallas as pl
from jax.experimental.pallas import tpu as pltpu
from jax.sharding import PartitionSpec as P

N = 256
BAND = 128
WIDTH = 512
FRAMES = 64
F_DEV = 2
REGIONS = 32
MODES = 16
Z = 16
Y = 4
SHARE = BAND // MODES
TURNS = 8
f32 = jnp.float32
bf16 = jnp.bfloat16

VMEM = pl.BlockSpec(memory_space=pltpu.VMEM)
SMEM = pl.BlockSpec(memory_space=pltpu.SMEM)
DMA = pltpu.SemaphoreType.DMA

NEAR = ((2, 1), (2, 0), (1, 1), (3, 1), (1, 0), (3, 0), (0, 1), (0, 0))
OTHERS = len(NEAR) - 1


def send(src, dst, send_sem, recv_sem, axis, index):
    copy = pltpu.make_async_remote_copy(
        src_ref=src,
        dst_ref=dst,
        send_sem=send_sem,
        recv_sem=recv_sem,
        device_id={axis: index},
        device_id_type=pl.DeviceIdType.MESH,
    )
    copy.start()
    return copy


def greet(peers):
    barrier = pltpu.get_barrier_semaphore()
    for axis, peer in peers:
        pl.semaphore_signal(
            barrier, inc=1, device_id={axis: peer}, device_id_type=pl.DeviceIdType.MESH
        )
    pl.semaphore_wait(barrier, len(peers))


class ModeGroup:
    def __init__(self):
        self.me = lax.axis_index("mode")
        self.y = self.me // 4
        self.x = (self.me // 2) % 2
        self.core = self.me % 2
        self.twin = self.me + 1 - 2 * self.core

    def chip(self, dy, dx):
        return ((self.y + dy) % Y) * 2 + (self.x + dx) % 2

    def chip_before(self, dy, dx):
        return ((self.y + Y - dy) % Y) * 2 + (self.x + 2 - dx) % 2

    def peers(self):
        chips = [2 * self.chip(dy, dx) + self.core for dy, dx in NEAR[:OTHERS]]
        return [("mode", peer) for peer in chips + [self.twin]]


def mode_scatter(group, x_ref, twin_buf, peer_buf, sems, copies):
    twin_send, twin_recv, peer_send, peer_recv = sems
    twin_copies = []
    for i, (dy, dx) in enumerate(NEAR):
        block = 2 * group.chip(dy, dx) + 1 - group.core
        twin_copies.append(
            send(x_ref.at[:, block], twin_buf.at[i], twin_send.at[i], twin_recv.at[i], "mode", group.twin)
        )
    yield
    peer_copies = []
    for i, (dy, dx) in enumerate(NEAR):
        target = 2 * group.chip(dy, dx) + group.core
        twin_copies[i].wait_recv()
        twin_buf[i] = twin_buf[i] + x_ref[:, target]
        if i < OTHERS:
            peer_copies.append(
                send(twin_buf.at[i], peer_buf.at[i], peer_send.at[i], peer_recv.at[i], "mode", target)
            )
    yield
    total = twin_buf[OTHERS]
    for i in reversed(range(OTHERS)):
        peer_copies[i].wait_recv()
        total = total + peer_buf[i]
    copies += twin_copies + peer_copies
    return total


def mode_gather(group, out_ref, sems, copies):
    twin_send, twin_recv, peer_send, peer_recv = sems
    mine = out_ref.at[:, group.me]
    peer_copies = []
    for i, (dy, dx) in enumerate(NEAR[:OTHERS]):
        target = 2 * group.chip(dy, dx) + group.core
        peer_copies.append(send(mine, mine, peer_send.at[i], peer_recv.at[i], "mode", target))
    twin_copies = [
        send(mine, mine, twin_send.at[OTHERS], twin_recv.at[OTHERS], "mode", group.twin)
    ]
    yield
    for i in reversed(range(OTHERS)):
        dy, dx = NEAR[i]
        block = out_ref.at[:, 2 * group.chip_before(dy, dx) + group.core]
        peer_copies[i].wait_recv()
        twin_copies.append(send(block, block, twin_send.at[i], twin_recv.at[i], "mode", group.twin))
    yield
    for copy in twin_copies:
        copy.wait_recv()
    copies += twin_copies + peer_copies


class RegionGroup:
    def __init__(self):
        self.me = lax.axis_index("region")
        self.x = self.me // Z
        self.z = self.me % Z
        self.partner = (1 - self.x) * Z + self.z

    def at(self, step):
        return self.x * Z + (self.z + step % Z) % Z

    def block(self, half, step):
        side = self.x if half == 1 else 1 - self.x
        return side * Z + (self.z + step % Z) % Z

    def peers(self):
        return [("region", self.block(half, step)) for half, step in ALL]


FAR = (8, 4, 12)
NEXT = (1, -1, 2, -2)


ALL = tuple(
    (half, step)
    for step in (8, 7, 9, 6, 10, 5, 11, 4, 12, 3, 13, 2, 14, 1, 15, 0)
    for half in ((0, 1) if step else (0,))
)


def neighbours(step):
    return NEXT if step % 8 == 0 else NEXT[:2]


def region_scatter(group, x_ref, near_buf, far_buf, side_buf, sems, copies):
    near_send, near_recv, far_send, far_recv, side_send, side_recv = sems
    near = {}
    far = {}
    for half in (0, 1):
        for e, step in enumerate((*FAR, 0)):
            for t, turn in enumerate(neighbours(step)):
                near[half, e, t] = send(
                    x_ref.at[:, group.block(half, turn + step)], near_buf.at[half, e, t],
                    near_send.at[half, e, t], near_recv.at[half, e, t], "region", group.at(turn),
                )
    yield
    for half in (0, 1):
        for e, step in enumerate((*FAR, 0)):
            total = x_ref[:, group.block(half, step)]
            for t in range(len(neighbours(step))):
                near[half, e, t].wait_recv()
                total = total + near_buf[half, e, t]
            near_buf[half, e, 0] = total
            if step:
                far[half, e] = send(
                    near_buf.at[half, e, 0], far_buf.at[half, e], far_send.at[half, e],
                    far_recv.at[half, e], "region", group.at(step),
                )
    yield
    side = None
    for half in (0, 1):
        total = near_buf[half, len(FAR), 0]
        for e in reversed(range(len(FAR))):
            far[half, e].wait_recv()
            total = total + far_buf[half, e]
        near_buf[half, len(FAR), 0] = total
        if half == 0:
            side = send(
                near_buf.at[half, len(FAR), 0], side_buf, side_send.at[0], side_recv.at[0],
                "region", group.partner,
            )
    yield
    side.wait_recv()
    copies += list(near.values()) + list(far.values()) + [side]
    return near_buf[1, len(FAR), 0] + side_buf[...]


def region_gather(group, out_ref, sems, copies):
    near_send, near_recv, far_send, far_recv, side_send, side_recv = sems
    near = {}
    far = {}
    mine = out_ref.at[:, group.me]
    side = send(mine, mine, side_send.at[0], side_recv.at[0], "region", group.partner)

    def go_near(half, e, step):
        block = out_ref.at[:, group.block(half, -step)]
        for t, turn in enumerate(neighbours(step)):
            near[half, e, t] = send(
                block, block, near_send.at[half, e, t], near_recv.at[half, e, t],
                "region", group.at(turn),
            )

    for half in (1, 0):
        block = out_ref.at[:, group.block(half, 0)]
        if half == 0:
            side.wait_recv()
        for e, step in enumerate(FAR):
            far[half, e] = send(
                block, block, far_send.at[half, e], far_recv.at[half, e], "region", group.at(step)
            )
        go_near(half, len(FAR), 0)
    yield
    for half in (1, 0):
        for e in reversed(range(len(FAR))):
            far[half, e].wait_recv()
            go_near(half, e, FAR[e])
    yield
    for copy in near.values():
        copy.wait_recv()
    copies += list(near.values()) + list(far.values()) + [side]


def region_exchange(group, x_ref, out_ref, sems, copies):
    send_sem, recv_sem = sems
    begun = []
    for i, (half, step) in enumerate(ALL):
        target = group.block(half, step)
        begun.append(
            send(
                x_ref.at[:, target], out_ref.at[:, group.me], send_sem.at[i], recv_sem.at[i],
                "region", target,
            )
        )
    out_ref[:, group.me] = x_ref[:, group.me]
    yield
    for copy in begun:
        copy.wait_recv()
    copies += begun


def run(steps):
    while True:
        try:
            next(steps)
        except StopIteration as end:
            return end.value


def advance(steps):
    next(steps)


def mode_buffers(a, rows, width):
    return [pltpu.VMEM((OTHERS + 1, a, rows, width), f32), pltpu.VMEM((OTHERS, a, rows, width), f32)]


def region_buffers(a, rows, width):
    return [
        pltpu.VMEM((2, 4, 4, a, rows, width), f32),
        pltpu.VMEM((2, 3, a, rows, width), f32),
        pltpu.VMEM((a, rows, width), f32),
    ]


MODE_SEMS = [DMA((OTHERS + 1,)), DMA((OTHERS + 1,)), DMA((OTHERS,)), DMA((OTHERS,))]
REGION_SEMS = [DMA((2, 4, 4)), DMA((2, 4, 4)), DMA((2, 3)), DMA((2, 3)), DMA((1,)), DMA((1,))]
EXCHANGE_SEMS = [DMA((len(ALL),)), DMA((len(ALL),))]


def own_band_of(owner_ref):
    region = lax.axis_index("region")
    found = 0
    for band in range(REGIONS):
        found = found + jnp.where(owner_ref[band] == region, band, 0)
    return found


def touching_frame(scan_ref, own_band, region):
    firsts = [scan_ref[region * F_DEV + frame, 0] for frame in range(F_DEV)]
    columns = [scan_ref[region * F_DEV + frame, 1] for frame in range(F_DEV)]
    gaps = [own_band - first // BAND for first in firsts]
    covers = [jnp.logical_and(gap >= 0, gap <= 2) for gap in gaps]
    first = jnp.where(covers[0], firsts[0], firsts[1])
    column = jnp.where(covers[0], columns[0], columns[1])
    return first, column, jnp.logical_or(covers[0], covers[1])


def prepare(scan_ref, owner_ref, object_ref, packed, table, bits):
    share = lax.axis_index("mode")
    own_band = own_band_of(owner_ref)

    @pl.loop(0, REGIONS)
    def _(region):
        _, column, _ = touching_frame(scan_ref, own_band, region)
        for plane in range(2):
            rows = pltpu.roll(object_ref[plane, share], (WIDTH - column) % WIDTH, 1)
            packed[plane, region] = rows[:, :N]

    numbers = lax.broadcasted_iota(jnp.int32, (SHARE, N), 0) + share * SHARE
    for frame in range(F_DEV):
        first = scan_ref[lax.axis_index("region") * F_DEV + frame, 0]
        anchor = first // BAND
        homes = [owner_ref[anchor + k] for k in range(3)]
        outer = jnp.where(numbers >= first - anchor * BAND, homes[0], homes[2])
        inner = jnp.full((SHARE, N), homes[1], jnp.int32)
        odd = jnp.full((SHARE, N), anchor % 2, jnp.int32) == 1
        table[frame * 2] = jnp.where(odd, inner, outer)
        table[frame * 2 + 1] = jnp.where(odd, outer, inner)
        for k in range(TURNS):
            bits[frame * TURNS + k] = jnp.full((1, N), first // 2**k % 2, jnp.int32)


def select_rows(table, bands, out_ref):
    share = lax.axis_index("mode")
    for frame in range(F_DEV):
        for half in range(2):
            homes = table[frame * 2 + half]
            rows = [bands[plane, 0] for plane in range(2)]
            for block in range(1, REGIONS):
                here = homes == block
                rows = [jnp.where(here, bands[plane, block], rows[plane]) for plane in range(2)]
            for plane in range(2):
                out_ref[(frame * 2 + plane) * 2 + half, share] = rows[plane]


def place_terms(table, terms, out_ref):
    for block in range(REGIONS):
        rows = [jnp.zeros((SHARE, N), f32) for plane in range(2)]
        for frame in range(F_DEV):
            for half in range(2):
                here = table[frame * 2 + half] == block
                rows = [
                    jnp.where(here, terms[(frame * 2 + plane) * 2 + half], rows[plane])
                    for plane in range(2)
                ]
        for plane in range(2):
            out_ref[plane, block] = rows[plane]


def turn_rows(values, bits, frame, back):
    for k in range(TURNS):
        here = jnp.broadcast_to(bits[frame * TURNS + k], (N, N)) == 1
        shift = N - 2**k if back else 2**k
        if shift % 8 == 0:
            rolled = [jnp.concatenate([v[N - shift:], v[:N - shift]], axis=0) for v in values]
        else:
            rolled = [pltpu.roll(v, shift, 0) for v in values]
        values = [jnp.where(here, r, v) for r, v in zip(rolled, values)]
    return values


def update_kernel(scan_ref, owner_ref, parts_ref, object_ref, power_ref, out_ref, tall, placed):
    share = lax.axis_index("mode")
    own_band = own_band_of(owner_ref)
    tall[0:BAND, :] = jnp.zeros((BAND, N), f32)
    tall[BAND:BAND + N, :] = power_ref[...]
    tall[BAND + N:, :] = jnp.zeros((BAND + SHARE, N), f32)
    placed[...] = jnp.zeros(placed.shape, f32)
    blank = jnp.zeros((SHARE, WIDTH - N), f32)

    @pl.loop(0, REGIONS)
    def _(region):
        first, column, covers = touching_frame(scan_ref, own_band, region)
        start = jnp.where(covers, BAND + own_band * BAND - first, 0) + share * SHARE
        base = pl.multiple_of(start // 8 * 8, 8)
        rows = pltpu.roll(tall[pl.ds(base, 2 * SHARE), :], (2 * SHARE - start % 8) % (2 * SHARE), 0)
        rows = jnp.where(covers, rows[:SHARE], 0.0)
        for k, part in enumerate((parts_ref[0, region], parts_ref[1, region], rows)):
            wide = pltpu.roll(jnp.concatenate([part, blank], axis=1), column, 1)
            placed[k] = placed[k] + wide

    scale = placed[2] + 1.0
    for plane in range(2):
        out_ref[plane] = object_ref[plane, share] + placed[plane] / scale


def gather_rows_kernel(x_ref, out_ref, *sems):
    group = ModeGroup()
    copies = []
    greet(group.peers())
    out_ref[:, group.me] = x_ref[...]
    run(mode_gather(group, out_ref, sems, copies))
    for copy in copies:
        copy.wait_send()


def split(x):
    high = x.astype(bf16)
    low = (x - high.astype(f32)).astype(bf16)
    return high, low


def transform(real, imag, tables, sign):
    ch, cl, sh, sl = tables
    cosine = jnp.concatenate([ch, ch, cl], axis=1)
    sine = jnp.concatenate([sh, sh, sl], axis=1)
    minus = -sine
    if sign < 0:
        left_real = jnp.concatenate([cosine, sine], axis=1)
        left_imag = jnp.concatenate([minus, cosine], axis=1)
    else:
        left_real = jnp.concatenate([cosine, minus], axis=1)
        left_imag = jnp.concatenate([sine, cosine], axis=1)
    rh, rl = split(real)
    ih, il = split(imag)
    stacked = jnp.concatenate([rh, rl, rh, ih, il, ih], axis=0)
    mid_real = jnp.dot(left_real, stacked, preferred_element_type=f32)
    mid_imag = jnp.dot(left_imag, stacked, preferred_element_type=f32)
    rh, rl = split(mid_real)
    ih, il = split(mid_imag)
    beside = jnp.concatenate([rh, rl, rh, ih, il, ih], axis=1)
    cosine = jnp.concatenate([ch, ch, cl], axis=0)
    sine = jnp.concatenate([sh, sh, sl], axis=0)
    minus = -sine
    if sign < 0:
        right_real = jnp.concatenate([cosine, sine], axis=0)
        right_imag = jnp.concatenate([minus, cosine], axis=0)
    else:
        right_real = jnp.concatenate([cosine, minus], axis=0)
        right_imag = jnp.concatenate([sine, cosine], axis=0)
    return (
        jnp.dot(beside, right_real, preferred_element_type=f32),
        jnp.dot(beside, right_imag, preferred_element_type=f32),
    )


def load_tables(tables_ref):
    return tuple(tables_ref[i] for i in range(4))


def blocks(value, count):
    return value.reshape(count, N // count, N)


def whole(ref, k):
    return ref[k].reshape(N, N)


def program(
    packed, table, bits, probe_ref, measured_ref, tables_ref, probe_out, arrived, mode_power,
    bands, turned, windows, waves, power, intensity, summed, gradient, terms, parts, *rest,
):
    rest = list(rest)

    def take(count):
        taken = rest[:count]
        del rest[:count]
        return taken

    mode = ModeGroup()
    region = RegionGroup()
    copies = []
    tables = load_tables(tables_ref)

    greet(mode.peers() + region.peers())
    run(region_exchange(region, packed, bands, take(2), copies))
    select_rows(table, bands, turned)
    run(mode_gather(mode, turned, take(4), copies))
    total = jnp.zeros((N, N), f32)
    for frame in range(F_DEV):
        values = [turned[k:k + 2].reshape(N, N) for k in (frame * 4, frame * 4 + 2)]
        for plane, value in enumerate(turn_rows(values, bits, frame, True)):
            windows[frame, plane] = value
            total = total + value * value
    power[0] = blocks(total, REGIONS)
    power_steps = region_scatter(region, power, *take(3), take(6), copies)
    advance(power_steps)

    def forward(frame, pr, pi):
        wr, wi = windows[frame, 0], windows[frame, 1]
        real, imag = transform(pr * wr - pi * wi, pr * wi + pi * wr, tables, -1)
        waves[frame, 0] = real
        waves[frame, 1] = imag
        intensity[frame] = blocks(real * real + imag * imag, MODES)

    def change(frame):
        factor = jnp.sqrt(measured_ref[frame]) / jnp.sqrt(whole(summed, frame) + 0.1) - 1.0
        return transform(waves[frame, 0] * factor, waves[frame, 1] * factor, tables, 1)

    pr, pi = whole(probe_ref, 0), whole(probe_ref, 1)
    forward(0, pr, pi)
    forward(1, pr, pi)
    first_two = (pl.ds(0, F_DEV),)
    sums = mode_scatter(mode, intensity.at[first_two], *take(2), take(4), copies)
    advance(sums)
    advance(power_steps)
    total = run(sums)
    for frame in range(F_DEV):
        summed[frame, mode.me] = total[frame]
    gathers = mode_gather(mode, summed.at[first_two], take(4), copies)
    advance(gathers)
    advance(power_steps)
    run(gathers)
    power_total = run(power_steps)
    grad_real = jnp.zeros((N, N), f32)
    grad_imag = jnp.zeros((N, N), f32)
    for frame in range(F_DEV):
        cr, ci = change(frame)
        wr, wi = windows[frame, 0], windows[frame, 1]
        grad_real = grad_real + (wr * cr + wi * ci)
        grad_imag = grad_imag + (wr * ci - wi * cr)
    gradient[0] = blocks(grad_real, REGIONS)
    gradient[1] = blocks(grad_imag, REGIONS)
    total = run(region_scatter(region, gradient, *take(3), take(6), copies))
    probe_out[:, region.me] = probe_ref[:, region.me] + total / (power_total + 1.0)
    run(region_gather(region, probe_out, take(6), copies))

    pr, pi = whole(probe_out, 0), whole(probe_out, 1)
    intensity_again, summed_again = take(2)
    intensity = intensity_again
    summed = summed_again
    forward(0, pr, pi)
    forward(1, pr, pi)
    intensity[F_DEV] = blocks(pr * pr + pi * pi, MODES)
    total = run(mode_scatter(mode, intensity, *take(2), take(4), copies))
    summed[:, mode.me] = total
    run(mode_gather(mode, summed, take(4), copies))
    for frame in range(F_DEV):
        cr, ci = change(frame)
        values = [pr * cr + pi * ci, pr * ci - pi * cr]
        for plane, value in enumerate(turn_rows(values, bits, frame, False)):
            k = frame * 4 + plane * 2
            terms[k:k + 2] = value.reshape(2, MODES, SHARE, N)
    total = run(mode_scatter(mode, terms, *take(2), take(4), copies))
    place_terms(table, total, parts)
    run(region_exchange(region, parts, arrived, take(2), copies))
    mode_power[...] = whole(summed, F_DEV)
    for copy in copies:
        copy.wait_send()


def vmem(*shape):
    return pltpu.VMEM(shape, f32)


SCRATCH = [
    vmem(2, REGIONS, SHARE, N),
    vmem(8, MODES, SHARE, N),
    vmem(F_DEV, 2, N, N),
    vmem(F_DEV, 2, N, N),
    vmem(1, REGIONS, 8, N),
    vmem(F_DEV, MODES, 16, N),
    vmem(F_DEV, MODES, 16, N),
    vmem(2, REGIONS, 8, N),
    vmem(8, MODES, SHARE, N),
    vmem(2, REGIONS, SHARE, N),
    *EXCHANGE_SEMS,
    *MODE_SEMS,
    *region_buffers(1, 8, N), *REGION_SEMS,
    *mode_buffers(F_DEV, 16, N), *MODE_SEMS,
    *MODE_SEMS,
    *region_buffers(2, 8, N), *REGION_SEMS,
    *REGION_SEMS,
    vmem(F_DEV + 1, MODES, 16, N), vmem(F_DEV + 1, MODES, 16, N),
    *mode_buffers(F_DEV + 1, 16, N), *MODE_SEMS,
    *MODE_SEMS,
    *mode_buffers(8, SHARE, N), *MODE_SEMS,
    *EXCHANGE_SEMS,
]


def call(kernel, name, outs, n_smem, args, scratch=(), collective_id=None):
    params = pltpu.CompilerParams(vmem_limit_bytes=60 * 2**20)
    if collective_id is not None:
        params = pltpu.CompilerParams(
            collective_id=collective_id, has_side_effects=True, vmem_limit_bytes=60 * 2**20
        )
    return pl.pallas_call(
        kernel,
        name=name,
        out_shape=[jax.ShapeDtypeStruct(*out) for out in outs],
        in_specs=[SMEM] * n_smem + [VMEM] * (len(args) - n_smem),
        out_specs=[VMEM] * len(outs),
        scratch_shapes=list(scratch),
        compiler_params=params,
    )(*args)


def body(measured, probe_modes, object_bands, scan_offsets, band_owner):
    shares = object_bands.reshape(2, MODES, SHARE, WIDTH)
    exchanged = ((2, REGIONS, SHARE, N), f32)
    packed, table, bits = call(
        prepare, "prepare",
        [exchanged, ((2 * F_DEV, SHARE, N), jnp.int32), ((F_DEV * TURNS, 1, N), jnp.int32)],
        2, [scan_offsets, band_owner, shares],
    )
    probe, arrived, power = call(
        program, "ptychography", [((2, REGIONS, 8, N), f32), exchanged, ((N, N), f32)], 0,
        [packed, table, bits, probe_modes.reshape(2, REGIONS, 8, N), measured, jnp.asarray(table_array())],
        SCRATCH, 1,
    )
    (rows,) = call(
        update_kernel, "update", [((2, SHARE, WIDTH), f32)], 2,
        [scan_offsets, band_owner, arrived, shares, power],
        [vmem(2 * BAND + N + SHARE, N), vmem(3, SHARE, WIDTH)],
    )
    (object_out,) = call(
        gather_rows_kernel, "gather_rows", [((2, MODES, SHARE, WIDTH), f32)], 0, [rows], MODE_SEMS, 2
    )
    return probe.reshape(2, 1, N, N), object_out.reshape(2, BAND, WIDTH)


def table_array():
    product = np.arange(N)[:, None] * np.arange(N)[None, :] % N
    angles = product * (2.0 * math.pi / N)
    pieces = []
    for values in (np.cos(angles) / 16.0, np.sin(angles) / 16.0):
        high = values.astype(bf16)
        pieces += [high, (values - high.astype(np.float64)).astype(bf16)]
    return np.stack(pieces)


def solution(mesh):
    in_specs = (
        P("region", None, None),
        P(None, "mode", None, None),
        P(None, "region", None),
        P(),
        P(),
    )
    out_specs = (P(None, "mode", None, None), P(None, "region", None))
    return jax.shard_map(body, mesh=mesh, in_specs=in_specs, out_specs=out_specs, check_vma=False)
```

time: 1180 us -> 193 us (0.16); the launches traced: 1160 us -> 192 us
  waiting for transfers between devices: 735 us -> 0 us
  Pallas kernels: 0 us -> 188 us
  other arithmetic: 177 us -> 0 us
  local copies, waits for them, and re-layouts: 119 us -> 3.4 us
  matrix products: 54.6 us -> 0 us
  starting transfers between devices: 33 us -> 0 us
  blocking collectives: 25 us -> 0 us
  between operations: 14.6 us -> 0.67 us
    psum x3 -> x0, waiting for transfers between devices: 566 us -> none  [the longest x1 281 us: body(): gradient, power_total = lax.psum((gradient, object_power), 'region')]
    pallas_call x0 -> x4, Pallas kernels: none -> 188 us  [call(): pl.pallas_call(kernel, name=name, out_shape=[jax.ShapeDtypeStruct(*out) f...]
    scatter x65 -> x0, other arithmetic: 166 us -> none
    scatter x96 -> x0, local copies, waits for them, and re-layouts: 73.8 us -> none
    all_to_all x2 -> x0, waiting for transfers between devices: 70.5 us -> none  [the longest x1 38.9 us: body(): lax.all_to_all(outgoing_update, 'region', split_axis=0, concat_axis=0, ti...]
    unnamed x6 -> x0, waiting for transfers between devices: 64.7 us -> none
    dot_general x26 -> x0, matrix products: 54.6 us -> none  [the longest x12 26.5 us: left_product(): return jnp.einsum('jk,...kl->...jl', matrix, planes, precision=highest)]
    all_gather x1 -> x0, waiting for transfers between devices: 34.2 us -> none  [body(): assembled = lax.all_gather(chosen, 'mode', axis=2, tiled=True)]
  transfers between devices with their start and end apart: 7 -> 0, of which waited for: 7 -> 0; matrix products, arithmetic and copies ran while one was open for 0% -> 0% of each run, Pallas kernels for 0% -> 0%
where the time goes in v2:
time: 193 us; the launch traced here: 192 us
  Pallas kernels  188 us (97%)
  local copies, waits for them, and re-layouts  3.4 us (2%)
    pallas_call x4, Pallas kernels, call(): pl.pallas_call(kernel, name=name, out_shape=[jax.ShapeDtypeStruct(*out) f...  188 us

profile of v2, /device:TPU:1, one launch (start us, length us, event | category | flops | bytes accessed | tf_op | source)
XLA Modules:
  0.0 192.2 jit_solution(16270787520216272212)
XLA Ops:
  0.6 0.0 copy-start.2
  0.6 0.7 copy-done.2
  1.3 0.7 copy.8.scan_ref
  2.0 4.7 %prepare.1 = (f32[2,32,8,256]{3,2,1,0:T(8,128)}, s32[4,8,256]{2,1,0:T(8,128)}, s32[16,1,256]{2,1,0:T(1,128)}) custom-call(s32[64,2]{1,0:T(8,128)} %copy.8.scan_ref, s32[32]{0:T(128)} %owner_ref.3, f32[2,16,8,512]{3,2,1,0:T(8,128)} %bitcast.6), custom_call_target="tpu_custom_call" | custom-call | tf_op jit(solution)/shard_map/prepare/pallas_call | solution.py:580
  6.7 167.2 %ptychography.1 = (f32[2,32,8,256]{3,2,1,0:T(8,128)}, f32[2,32,8,256]{3,2,1,0:T(8,128)}, f32[256,256]{1,0:T(8,128)}) custom-call(f32[2,32,8,256]{3,2,1,0:T(8,128)} %get-tuple-element.8.packed, s32[4,8,256]{2,1,0:T(8,128)} %get-tuple-element.9.table, s32[16,1,256]{2,1,0:T(1,128)} %get-tuple-element.10.bits, f32[2,32,8,256]{3,2,1,0:T(8,128)} %bitcast.10, ...), custom_call_target="tpu_custom_call" | custom-call | tf_op jit(solution)/shard_map/ptychography/pallas_call | solution.py:580
  173.9 5.0 %update.1.x_ref = f32[2,8,512]{2,1,0:T(8,128)} custom-call(s32[64,2]{1,0:T(8,128)} %copy.8.scan_ref, s32[32]{0:T(128)} %owner_ref.3, f32[2,32,8,256]{3,2,1,0:T(8,128)} %get-tuple-element.12.parts_ref, f32[2,16,8,512]{3,2,1,0:T(8,128)} %bitcast.7, f32[256,256]{1,0:T(8,128)} %get-tuple-element.13.power_ref), custom_call_target="tpu_custom_call" | custom-call | tf_op jit(solution)/shard_map/update/pallas_call | solution.py:580
  178.9 0.0 copy-start.1
  178.9 11.3 %gather_rows.1 = f32[2,16,8,512]{3,2,1,0:T(8,128)} custom-call(f32[2,8,512]{2,1,0:T(8,128)} %update.1.x_ref), custom_call_target="tpu_custom_call" | custom-call | tf_op jit(solution)/shard_map/gather_rows/pallas_call | solution.py:580
  190.2 0.0 copy-done.1
  190.2 0.0 copy-start
  190.2 0.8 copy.13
  191.0 0.4 copy-done
  191.4 0.8 copy.14
Async XLA Ops:
  0.6 0.7 copy-start.2
  178.9 11.3 %copy-start.1 = (f32[2,32,8,256]{3,2,1,0:T(8,128)S(1)}, f32[2,32,8,256]{3,2,1,0:T(8,128)}, u32[]{:S(2)}) copy-start(f32[2,32,8,256]{3,2,1,0:T(8,128)} %get-tuple-element.11) | copy-start | bytes 1572868
  190.2 1.2 copy-start

commit v3 on v2

--- a/solution.py
+++ b/solution.py
@@ -301,7 +301,7 @@
     share = lax.axis_index("mode")
     own_band = own_band_of(owner_ref)
 
-    @pl.loop(0, REGIONS)
+    @pl.loop(0, REGIONS, unroll=8)
     def _(region):
         _, column, _ = touching_frame(scan_ref, own_band, region)
         for plane in range(2):
@@ -322,31 +322,22 @@
             bits[frame * TURNS + k] = jnp.full((1, N), first // 2**k % 2, jnp.int32)
 
 
-def select_rows(table, bands, out_ref):
+def select_rows(table, bands, plane, out_ref):
     share = lax.axis_index("mode")
-    for frame in range(F_DEV):
-        for half in range(2):
-            homes = table[frame * 2 + half]
-            rows = [bands[plane, 0] for plane in range(2)]
-            for block in range(1, REGIONS):
-                here = homes == block
-                rows = [jnp.where(here, bands[plane, block], rows[plane]) for plane in range(2)]
-            for plane in range(2):
-                out_ref[(frame * 2 + plane) * 2 + half, share] = rows[plane]
-
-
-def place_terms(table, terms, out_ref):
+    for k in range(2 * F_DEV):
+        homes = table[k]
+        rows = bands[plane, 0]
+        for block in range(1, REGIONS):
+            rows = jnp.where(homes == block, bands[plane, block], rows)
+        out_ref[plane * 2 * F_DEV + k, share] = rows
+
+
+def place_terms(table, terms, plane, out_ref):
     for block in range(REGIONS):
-        rows = [jnp.zeros((SHARE, N), f32) for plane in range(2)]
-        for frame in range(F_DEV):
-            for half in range(2):
-                here = table[frame * 2 + half] == block
-                rows = [
-                    jnp.where(here, terms[(frame * 2 + plane) * 2 + half], rows[plane])
-                    for plane in range(2)
-                ]
-        for plane in range(2):
-            out_ref[plane, block] = rows[plane]
+        rows = jnp.zeros((SHARE, N), f32)
+        for k in range(2 * F_DEV):
+            rows = jnp.where(table[k] == block, terms[k], rows)
+        out_ref[plane, block] = rows
 
 
 def turn_rows(values, bits, frame, back):
@@ -370,7 +361,7 @@
     placed[...] = jnp.zeros(placed.shape, f32)
     blank = jnp.zeros((SHARE, WIDTH - N), f32)
 
-    @pl.loop(0, REGIONS)
+    @pl.loop(0, REGIONS, unroll=8)
     def _(region):
         first, column, covers = touching_frame(scan_ref, own_band, region)
         start = jnp.where(covers, BAND + own_band * BAND - first, 0) + share * SHARE
@@ -465,12 +456,24 @@
     tables = load_tables(tables_ref)
 
     greet(mode.peers() + region.peers())
-    run(region_exchange(region, packed, bands, take(2), copies))
-    select_rows(table, bands, turned)
-    run(mode_gather(mode, turned, take(4), copies))
+    exchanges = []
+    for plane in range(2):
+        part = (pl.ds(plane, 1),)
+        exchanges.append(region_exchange(region, packed.at[part], bands.at[part], take(2), copies))
+        advance(exchanges[plane])
+    gathers = []
+    for plane in range(2):
+        run(exchanges[plane])
+        select_rows(table, bands, plane, turned)
+        part = (pl.ds(plane * 2 * F_DEV, 2 * F_DEV),)
+        gathers.append(mode_gather(mode, turned.at[part], take(4), copies))
+        advance(gathers[plane])
+        advance(gathers[plane])
+    run(gathers[0])
+    run(gathers[1])
     total = jnp.zeros((N, N), f32)
     for frame in range(F_DEV):
-        values = [turned[k:k + 2].reshape(N, N) for k in (frame * 4, frame * 4 + 2)]
+        values = [turned[k:k + 2].reshape(N, N) for k in (frame * 2, (F_DEV + frame) * 2)]
         for plane, value in enumerate(turn_rows(values, bits, frame, True)):
             windows[frame, plane] = value
             total = total + value * value
@@ -518,12 +521,16 @@
     run(region_gather(region, probe_out, take(6), copies))
 
     pr, pi = whole(probe_out, 0), whole(probe_out, 1)
+    strength, strength_sum = take(2)
+    strength[0] = blocks(pr * pr + pi * pi, MODES)
+    strengths = mode_scatter(mode, strength, *take(2), take(4), copies)
+    strength_gathers = mode_gather(mode, strength_sum, take(4), copies)
+    advance(strengths)
     intensity_again, summed_again = take(2)
     intensity = intensity_again
     summed = summed_again
     forward(0, pr, pi)
     forward(1, pr, pi)
-    intensity[F_DEV] = blocks(pr * pr + pi * pi, MODES)
     total = run(mode_scatter(mode, intensity, *take(2), take(4), copies))
     summed[:, mode.me] = total
     run(mode_gather(mode, summed, take(4), copies))
@@ -531,12 +538,27 @@
         cr, ci = change(frame)
         values = [pr * cr + pi * ci, pr * ci - pi * cr]
         for plane, value in enumerate(turn_rows(values, bits, frame, False)):
-            k = frame * 4 + plane * 2
+            k = (plane * F_DEV + frame) * 2
             terms[k:k + 2] = value.reshape(2, MODES, SHARE, N)
-    total = run(mode_scatter(mode, terms, *take(2), take(4), copies))
-    place_terms(table, total, parts)
-    run(region_exchange(region, parts, arrived, take(2), copies))
-    mode_power[...] = whole(summed, F_DEV)
+    scatters = []
+    for plane in range(2):
+        part = (pl.ds(plane * 2 * F_DEV, 2 * F_DEV),)
+        scatters.append(mode_scatter(mode, terms.at[part], *take(2), take(4), copies))
+        advance(scatters[plane])
+    advance(scatters[0])
+    advance(scatters[1])
+    exchanges = []
+    for plane in range(2):
+        place_terms(table, run(scatters[plane]), plane, parts)
+        part = (pl.ds(plane, 1),)
+        exchanges.append(region_exchange(region, parts.at[part], arrived.at[part], take(2), copies))
+        advance(exchanges[plane])
+    advance(strengths)
+    strength_sum[:, mode.me] = run(strengths)
+    run(strength_gathers)
+    mode_power[...] = whole(strength_sum, 0)
+    run(exchanges[0])
+    run(exchanges[1])
     for copy in copies:
         copy.wait_send()
 
@@ -556,18 +578,22 @@
     vmem(2, REGIONS, 8, N),
     vmem(8, MODES, SHARE, N),
     vmem(2, REGIONS, SHARE, N),
-    *EXCHANGE_SEMS,
-    *MODE_SEMS,
+    *EXCHANGE_SEMS, *EXCHANGE_SEMS,
+    *MODE_SEMS, *MODE_SEMS,
     *region_buffers(1, 8, N), *REGION_SEMS,
     *mode_buffers(F_DEV, 16, N), *MODE_SEMS,
     *MODE_SEMS,
     *region_buffers(2, 8, N), *REGION_SEMS,
     *REGION_SEMS,
-    vmem(F_DEV + 1, MODES, 16, N), vmem(F_DEV + 1, MODES, 16, N),
-    *mode_buffers(F_DEV + 1, 16, N), *MODE_SEMS,
+    vmem(1, MODES, 16, N), vmem(1, MODES, 16, N),
+    *mode_buffers(1, 16, N), *MODE_SEMS,
     *MODE_SEMS,
-    *mode_buffers(8, SHARE, N), *MODE_SEMS,
-    *EXCHANGE_SEMS,
+    vmem(F_DEV, MODES, 16, N), vmem(F_DEV, MODES, 16, N),
+    *mode_buffers(F_DEV, 16, N), *MODE_SEMS,
+    *MODE_SEMS,
+    *mode_buffers(2 * F_DEV, SHARE, N), *MODE_SEMS,
+    *mode_buffers(2 * F_DEV, SHARE, N), *MODE_SEMS,
+    *EXCHANGE_SEMS, *EXCHANGE_SEMS,
 ]
 
 

time: 193 us -> 184 us (0.953)
  Pallas kernels: 188 us -> 180 us
    pallas_call x4, Pallas kernels: 188 us -> 180 us  [call(): pl.pallas_call(kernel, name=name, out_shape=[jax.ShapeDtypeStruct(*out) f...]
where the time goes in v3:
time: 184 us
  Pallas kernels  180 us (98%)
  local copies, waits for them, and re-layouts  3.4 us (2%)
    pallas_call x4, Pallas kernels, call(): pl.pallas_call(kernel, name=name, out_shape=[jax.ShapeDtypeStruct(*out) f...  180 us

profile of v3, /device:TPU:1, one launch (start us, length us, event | category | flops | bytes accessed | tf_op | source)
XLA Modules:
  0.0 183.9 jit_solution(16150846477703043133)
XLA Ops:
  0.6 0.0 copy-start.2
  0.6 0.7 copy-done.2
  1.3 0.7 copy.8.scan_ref
  2.0 2.8 %prepare.1 = (f32[2,32,8,256]{3,2,1,0:T(8,128)}, s32[4,8,256]{2,1,0:T(8,128)}, s32[16,1,256]{2,1,0:T(1,128)}) custom-call(s32[64,2]{1,0:T(8,128)} %copy.8.scan_ref, s32[32]{0:T(128)} %owner_ref.3, f32[2,16,8,512]{3,2,1,0:T(8,128)} %bitcast.6), custom_call_target="tpu_custom_call" | custom-call | tf_op jit(solution)/shard_map/prepare/pallas_call | solution.py:606
  4.8 162.6 %ptychography.1 = (f32[2,32,8,256]{3,2,1,0:T(8,128)}, f32[2,32,8,256]{3,2,1,0:T(8,128)}, f32[256,256]{1,0:T(8,128)}) custom-call(f32[2,32,8,256]{3,2,1,0:T(8,128)} %get-tuple-element.8.packed, s32[4,8,256]{2,1,0:T(8,128)} %get-tuple-element.9.table, s32[16,1,256]{2,1,0:T(1,128)} %get-tuple-element.10.bits, f32[2,32,8,256]{3,2,1,0:T(8,128)} %bitcast.10, ...), custom_call_target="tpu_custom_call" | custom-call | tf_op jit(solution)/shard_map/ptychography/pallas_call | solution.py:606
  167.4 3.2 %update.1.x_ref = f32[2,8,512]{2,1,0:T(8,128)} custom-call(s32[64,2]{1,0:T(8,128)} %copy.8.scan_ref, s32[32]{0:T(128)} %owner_ref.3, f32[2,32,8,256]{3,2,1,0:T(8,128)} %get-tuple-element.12.parts_ref, f32[2,16,8,512]{3,2,1,0:T(8,128)} %bitcast.7, f32[256,256]{1,0:T(8,128)} %get-tuple-element.13.power_ref), custom_call_target="tpu_custom_call" | custom-call | tf_op jit(solution)/shard_map/update/pallas_call | solution.py:606
  170.6 0.0 copy-start.1
  170.6 11.3 %gather_rows.1 = f32[2,16,8,512]{3,2,1,0:T(8,128)} custom-call(f32[2,8,512]{2,1,0:T(8,128)} %update.1.x_ref), custom_call_target="tpu_custom_call" | custom-call | tf_op jit(solution)/shard_map/gather_rows/pallas_call | solution.py:606
  181.9 0.0 copy-done.1
  181.9 0.0 copy-start
  181.9 0.8 copy.13
  182.7 0.4 copy-done
  183.1 0.8 copy.14
Async XLA Ops:
  0.6 0.7 copy-start.2
  170.6 11.3 %copy-start.1 = (f32[2,32,8,256]{3,2,1,0:T(8,128)S(1)}, f32[2,32,8,256]{3,2,1,0:T(8,128)}, u32[]{:S(2)}) copy-start(f32[2,32,8,256]{3,2,1,0:T(8,128)} %get-tuple-element.11) | copy-start | bytes 1572868
  181.9 1.2 copy-start

commit v4 on v3

--- a/solution.py
+++ b/solution.py
@@ -176,25 +176,23 @@
             if step:
                 far[half, e] = send(
                     near_buf.at[half, e, 0], far_buf.at[half, e], far_send.at[half, e],
-                    far_recv.at[half, e], "region", group.at(step),
+                    far_recv.at[half, e], "region", group.block(half, step),
                 )
-    yield
-    side = None
-    for half in (0, 1):
-        total = near_buf[half, len(FAR), 0]
-        for e in reversed(range(len(FAR))):
+            elif half == 0:
+                side = send(
+                    near_buf.at[half, e, 0], side_buf, side_send.at[0], side_recv.at[0],
+                    "region", group.partner,
+                )
+    yield
+    side.wait_recv()
+    total = near_buf[1, len(FAR), 0] + side_buf[...]
+    for e in reversed(range(len(FAR))):
+        for half in (0, 1):
             far[half, e].wait_recv()
             total = total + far_buf[half, e]
-        near_buf[half, len(FAR), 0] = total
-        if half == 0:
-            side = send(
-                near_buf.at[half, len(FAR), 0], side_buf, side_send.at[0], side_recv.at[0],
-                "region", group.partner,
-            )
-    yield
-    side.wait_recv()
     copies += list(near.values()) + list(far.values()) + [side]
-    return near_buf[1, len(FAR), 0] + side_buf[...]
+    yield
+    return total
 
 
 def region_gather(group, out_ref, sems, copies):
@@ -212,15 +210,15 @@
                 "region", group.at(turn),
             )
 
-    for half in (1, 0):
-        block = out_ref.at[:, group.block(half, 0)]
-        if half == 0:
-            side.wait_recv()
-        for e, step in enumerate(FAR):
+    for e, step in enumerate(FAR):
+        for half in (0, 1):
             far[half, e] = send(
-                block, block, far_send.at[half, e], far_recv.at[half, e], "region", group.at(step)
+                mine, mine, far_send.at[half, e], far_recv.at[half, e],
+                "region", group.block(half, step),
             )
-        go_near(half, len(FAR), 0)
+    go_near(1, len(FAR), 0)
+    side.wait_recv()
+    go_near(0, len(FAR), 0)
     yield
     for half in (1, 0):
         for e in reversed(range(len(FAR))):

time: 184 us -> 182 us (0.989)
  Pallas kernels: 180 us -> 178 us
    pallas_call x4, Pallas kernels: 180 us -> 178 us  [call(): pl.pallas_call(kernel, name=name, out_shape=[jax.ShapeDtypeStruct(*out) f...]
where the time goes in v4:
time: 182 us
  Pallas kernels  178 us (98%)
  local copies, waits for them, and re-layouts  3.4 us (2%)
    pallas_call x4, Pallas kernels, call(): pl.pallas_call(kernel, name=name, out_shape=[jax.ShapeDtypeStruct(*out) f...  178 us

profile of v4, /device:TPU:1, one launch (start us, length us, event | category | flops | bytes accessed | tf_op | source)
XLA Modules:
  0.0 181.6 jit_solution(14331364587810894527)
XLA Ops:
  0.6 0.0 copy-start.2
  0.6 0.7 copy-done.2
  1.3 0.7 copy.8.scan_ref
  2.0 2.8 %prepare.1 = (f32[2,32,8,256]{3,2,1,0:T(8,128)}, s32[4,8,256]{2,1,0:T(8,128)}, s32[16,1,256]{2,1,0:T(1,128)}) custom-call(s32[64,2]{1,0:T(8,128)} %copy.8.scan_ref, s32[32]{0:T(128)} %owner_ref.3, f32[2,16,8,512]{3,2,1,0:T(8,128)} %bitcast.6), custom_call_target="tpu_custom_call" | custom-call | tf_op jit(solution)/shard_map/prepare/pallas_call | solution.py:604
  4.8 160.5 %ptychography.1 = (f32[2,32,8,256]{3,2,1,0:T(8,128)}, f32[2,32,8,256]{3,2,1,0:T(8,128)}, f32[256,256]{1,0:T(8,128)}) custom-call(f32[2,32,8,256]{3,2,1,0:T(8,128)} %get-tuple-element.8.packed, s32[4,8,256]{2,1,0:T(8,128)} %get-tuple-element.9.table, s32[16,1,256]{2,1,0:T(1,128)} %get-tuple-element.10.bits, f32[2,32,8,256]{3,2,1,0:T(8,128)} %bitcast.10, ...), custom_call_target="tpu_custom_call" | custom-call | tf_op jit(solution)/shard_map/ptychography/pallas_call | solution.py:604
  165.3 3.2 %update.1.x_ref = f32[2,8,512]{2,1,0:T(8,128)} custom-call(s32[64,2]{1,0:T(8,128)} %copy.8.scan_ref, s32[32]{0:T(128)} %owner_ref.3, f32[2,32,8,256]{3,2,1,0:T(8,128)} %get-tuple-element.12.parts_ref, f32[2,16,8,512]{3,2,1,0:T(8,128)} %bitcast.7, f32[256,256]{1,0:T(8,128)} %get-tuple-element.13.power_ref), custom_call_target="tpu_custom_call" | custom-call | tf_op jit(solution)/shard_map/update/pallas_call | solution.py:604
  168.5 0.0 copy-start.1
  168.5 11.1 %gather_rows.1 = f32[2,16,8,512]{3,2,1,0:T(8,128)} custom-call(f32[2,8,512]{2,1,0:T(8,128)} %update.1.x_ref), custom_call_target="tpu_custom_call" | custom-call | tf_op jit(solution)/shard_map/gather_rows/pallas_call | solution.py:604
  179.6 0.0 copy-done.1
  179.6 0.0 copy-start
  179.6 0.8 copy.13
  180.4 0.4 copy-done
  180.8 0.8 copy.14
Async XLA Ops:
  0.6 0.7 copy-start.2
  168.5 11.1 %copy-start.1 = (f32[2,32,8,256]{3,2,1,0:T(8,128)S(1)}, f32[2,32,8,256]{3,2,1,0:T(8,128)}, u32[]{:S(2)}) copy-start(f32[2,32,8,256]{3,2,1,0:T(8,128)} %get-tuple-element.11) | copy-start | bytes 1572868
  179.6 1.2 copy-start
